TPU v7x, 128 devices: a whole 4x4x4 slice. The times are simulated.
128 devices in a mesh: segment: 2 (over x_lo), seq: 16 (over z, y), mp: 4 (over x_hi, core).
Axes of the slice: x: 4 (x_hi: 2, x_lo: 2; x = x_hi * 2 + x_lo), y: 4, z: 4, core: 2. Of those that a mesh axis runs over, the one named last changes fastest.
Arguments:
- memory: bfloat16 [2, 4096, 4096], P(None, 'seq', 'mp')
- decoder_rows: bfloat16 [2, 1024, 4096], P(None, 'seq', 'mp')
- gains: bfloat16 [2, 4096], P('segment'), may hold values from 0.5 to 1.5
- weights: bfloat16 [2, 2, 4096, 4096], P('segment', None, None, 'mp')
- lengths: int32 [2], replicated, may hold values from 512 to 4096, as said below
Outputs:
- decoder_out: bfloat16 [2, 1024, 4096], P(None, 'seq', ('segment', 'mp'))
Inputs may be any that keep to these rules, and one draw needn't show every extreme that they name: memory positions of document b at or beyond lengths[b] are padding; some document has all 4096 positions.
All inputs are finite; a program needn't handle non-finite values.
Results may differ from a plain program's by a relative error of at most 0.015.
The roundings to bfloat16 on the way count: a program that leaves them out, or rounds other values in their place, can miss the bound.
Values may be sent and summed in bfloat16 or wider, within the bound.
A program may use at most 192 MiB of HBM per device.

v0:
```python
import jax
import jax.numpy as jnp
from jax import lax
from jax.sharding import PartitionSpec as P

DKV = 64


norm_eps = 1e-06
masked_score = -1e30


def passed_along(shard, axis, by):
    count = lax.axis_size(axis)
    pairs = [(i, i + by) for i in range(count) if 0 <= i + by < count]
    return lax.ppermute(shard, axis, pairs)


def rms_rows(rows, gain):
    wide = rows.astype(jnp.float32)
    inverse = lax.rsqrt(jnp.mean(wide * wide, axis=1, keepdims=True) + norm_eps)
    return (wide * inverse * gain.astype(jnp.float32)[None, :]).astype(jnp.bfloat16)


def fold_block(running, queries, key_block, value_block, first_pos, lengths):
    maxima, totals, summed = running
    doc_count, span = (key_block.shape[0], key_block.shape[1])
    heads_here = queries.shape[2]
    key_heads = key_block.reshape(doc_count, span, heads_here, DKV)
    value_heads = value_block.reshape(doc_count, span, heads_here, DKV)
    scores = jnp.einsum("bqhd,bkhd->bhqk", queries, key_heads, preferred_element_type=jnp.float32)
    positions = first_pos + lax.iota(jnp.int32, span)
    valid_keys = (positions[None, :] < lengths[:, None])[:, None, None, :]
    masked = jnp.where(valid_keys, scores, masked_score)
    new_max = jnp.maximum(maxima, jnp.max(masked, axis=-1))
    exp_scores = jnp.where(valid_keys, jnp.exp(masked - new_max[..., None]), 0.0)
    rescale = jnp.exp(maxima - new_max)
    totals = totals * rescale + jnp.sum(exp_scores, axis=-1)
    summed = summed * rescale[..., None] + jnp.einsum(
        "bhqk,bkhd->bhqd",
        exp_scores.astype(jnp.bfloat16),
        value_heads,
        preferred_element_type=jnp.float32,
    )
    return (new_max, totals, summed)


def on_device(memory, decoder_rows, gains, weights, lengths):
    segment_index = lax.axis_index("segment")
    decoding = segment_index == 1
    doc_count, mem_dev, part_width = memory.shape
    pos_dev = decoder_rows.shape[1]
    mem_count = doc_count * mem_dev
    row_count = doc_count * pos_dev
    mem_full, dec_full = (
        lax.all_gather(memory.reshape(mem_count, part_width), "mp", axis=1, tiled=True),
        lax.all_gather(decoder_rows.reshape(row_count, part_width), "mp", axis=1, tiled=True),
    )
    first_weight = weights[0, 0]
    second_weight = weights[0, 1]
    section_gain = gains[0]
    head_width = first_weight.shape[1]
    heads_here = head_width // DKV

    def encode(source):
        normed = rms_rows(source, section_gain)
        key_out = jnp.dot(normed, first_weight, preferred_element_type=jnp.float32).astype(
            jnp.bfloat16
        )
        value_out = jnp.dot(normed, second_weight, preferred_element_type=jnp.float32).astype(
            jnp.bfloat16
        )
        return (key_out, value_out)

    def skip_encode(source):
        empty = jnp.zeros((mem_count, head_width), jnp.bfloat16)
        return (empty, empty)

    key_local, value_local = lax.cond(decoding, skip_encode, encode, mem_full)
    query_rows = lax.cond(
        decoding,
        lambda source: jnp.dot(
            rms_rows(source, section_gain), first_weight, preferred_element_type=jnp.float32
        ).astype(jnp.bfloat16),
        lambda source: jnp.zeros((row_count, head_width), jnp.bfloat16),
        dec_full,
    )
    key_rows, value_rows = passed_along((key_local, value_local), "segment", 1)
    key_flat = key_rows.reshape(doc_count, mem_dev, head_width)
    value_flat = value_rows.reshape(doc_count, mem_dev, head_width)
    queries = query_rows.reshape(doc_count, pos_dev, heads_here, DKV)
    start_state = (
        jnp.full((doc_count, heads_here, pos_dev), masked_score, jnp.float32),
        jnp.zeros((doc_count, heads_here, pos_dev), jnp.float32),
        jnp.zeros((doc_count, heads_here, pos_dev, DKV), jnp.float32),
    )
    first_pos = jnp.int32(0)
    key_part = lax.all_gather(key_flat, "seq", axis=1, tiled=True)
    value_part = lax.all_gather(value_flat, "seq", axis=1, tiled=True)
    span = key_part.shape[1]
    width = 256

    def attend(state):
        for offset in range(0, span, width):
            state = fold_block(
                state,
                queries,
                key_part[:, offset : offset + width],
                value_part[:, offset : offset + width],
                first_pos + offset,
                lengths,
            )
        return state

    final_state = lax.cond(decoding, attend, lambda state: state, start_state)

    def finish(state):
        context = state[2] / state[1][..., None]
        return (
            jnp.transpose(context, (0, 2, 1, 3)).reshape(row_count, head_width).astype(jnp.bfloat16)
        )

    context_rows = lax.cond(
        decoding,
        finish,
        lambda state: jnp.zeros((row_count, head_width), jnp.bfloat16),
        final_state,
    )
    update_terms = lax.cond(
        decoding,
        lambda source: lax.dot_general(
            source, second_weight, (((1,), (1,)), ((), ())), preferred_element_type=jnp.float32
        ),
        lambda source: jnp.zeros((row_count, second_weight.shape[0]), jnp.float32),
        context_rows,
    )
    update = lax.psum_scatter(
        update_terms.astype(jnp.bfloat16), ("segment", "mp"), scatter_dimension=1, tiled=True
    ).astype(jnp.float32)
    out_width = update.shape[1]
    group_index = segment_index * lax.axis_size("mp") + lax.axis_index("mp")
    residual = lax.dynamic_slice_in_dim(dec_full, group_index * out_width, out_width, 1)
    decoder_out = (residual.astype(jnp.float32) + update).astype(jnp.bfloat16)
    return decoder_out.reshape(doc_count, pos_dev, out_width)


def solution(mesh):
    in_specs = (
        P(None, "seq", "mp"),
        P(None, "seq", "mp"),
        P("segment", None),
        P("segment", None, None, "mp"),
        P(),
    )
    out_specs = P(None, "seq", ("segment", "mp"))
    return jax.shard_map(
        on_device, mesh=mesh, in_specs=in_specs, out_specs=out_specs, check_vma=False
    )
```

profile of v0, /device:TPU:7, one launch (start us, length us, event | category | flops | bytes accessed | tf_op | source)
XLA Modules:
  0.0 468.2 jit_solution(12025478866281575327)
XLA Ops:
  8.1 11.7 %slice_bitcast_fusion = (bf16[4096,1024]{1,0:T(8,128)(2,1)}, bf16[4096,1024]{1,0:T(8,128)(2,1)}) fusion(bf16[1,2,4096,1024]{3,2,1,0:T(8,128)(2,1)} %param.18), kind=kLoop, calls=%fused_computation.292 | loop fusion | bytes 33554432 | tf_op jit(solution)/shard_map/squeeze | solution.py:60
  19.8 28.9 %all-gather.7.cloned.1.call-done = bf16[512,4096]{1,0:T(8,128)(2,1)} async-done(((bf16[512,1024]{1,0:T(8,128)(2,1)}), bf16[512,4096]{1,0:T(8,128)(2,1)}) %all-gather.7.cloned.1.call-update) | async-done | bytes 4194320 | tf_op jit(solution)/shard_map/all_gather | solution.py:56
  50.3 40.4 %collective-permute-done = bf16[512,1024]{1,0:T(8,128)(2,1)S(1)} collective-permute-done((bf16[512,1024]{1,0:T(8,128)(2,1)S(1)}, bf16[512,1024]{1,0:T(8,128)(2,1)S(1)}, u32[]{:S(2)}, u32[]{:S(2)}) %collective-permute-start) | collective-permute-done | bytes 1048608 | tf_op jit(solution)/shard_map/ppermute | solution.py:16
  93.1 24.9 %collective-permute-done.1 = bf16[512,1024]{1,0:T(8,128)(2,1)S(1)} collective-permute-done((bf16[512,1024]{1,0:T(8,128)(2,1)S(1)}, bf16[512,1024]{1,0:T(8,128)(2,1)S(1)}, u32[]{:S(2)}, u32[]{:S(2)}) %collective-permute-start.1) | collective-permute-done | bytes 1048608 | tf_op jit(solution)/shard_map/ppermute | solution.py:16
  119.1 7.0 %conditional.6 = (bf16[2,64,16,64]{3,2,1,0:T(8,128)(2,1)S(1)}) conditional(s32[]{:T(128)} %convert_element_type.104, () %tuple.45, (bf16[128,4096]{1,0:T(8,128)(2,1)}, bf16[4096]{0:T(1024)(128)(2,1)S(1)}, bf16[4096,1024]{1,0:T(8,128)(2,1)}) %tuple.46), branch_computations={%region_3.0_spmd, %region_4.0_spmd} | conditional | flops 1077547136 | bytes 11315208 | solution.py:80
  119.1 1.5 fusion.5
  120.7 5.0 %convolution_convert_fusion.2 = bf16[128,1024]{1,0:T(8,128)(2,1)S(1)} fusion(bf16[4096,1024]{1,0:T(8,128)(2,1)} %get-tuple-element.51, bf16[128,4096]{1,0:T(8,128)(2,1)} %get-tuple-element.49, f32[4096]{0:T(1024)S(1)} %convert_element_type.76, f32[128]{0:T(128)S(1)} %add_rsqrt_fusion.1), kind=kOutput, calls=%fused_computation.13 | convolution fusion | flops 1075970048 | bytes 9716224 | tf_op jit(solution)/shard_map/cond/branch_1_fun/dot_general | solution.py:82
  126.1 78.8 %all-gather.9.cloned.1.call-done = bf16[2,4096,1024]{2,1,0:T(8,128)(2,1)} async-done(((bf16[2,256,1024]{2,1,0:T(8,128)(2,1)}), bf16[2,4096,1024]{2,1,0:T(8,128)(2,1)}) %all-gather.9.cloned.1.call-update) | async-done | bytes 16777232 | tf_op jit(solution)/shard_map/all_gather | solution.py:98
  204.9 113.1 %all-gather.11.cloned.1.call-done = bf16[2,4096,1024]{2,1,0:T(8,128)(2,1)} async-done(((bf16[2,256,1024]{2,1,0:T(8,128)(2,1)}), bf16[2,4096,1024]{2,1,0:T(8,128)(2,1)}) %all-gather.11.cloned.1.call-update) | async-done | bytes 16777232 | tf_op jit(solution)/shard_map/all_gather | solution.py:99
  318.0 100.6 %conditional.7 = (f32[2,16,64]{2,1,0:T(8,128)S(1)}, f32[2,16,64,64]{3,2,1,0:T(8,128)}) conditional(s32[]{:T(128)} %convert_element_type.104, () %tuple.42, (s32[2]{0:T(128)S(1)}, bf16[2,4096,1024]{2,1,0:T(8,128)(2,1)}, bf16[2,64,16,64]{3,2,1,0:T(8,128)(2,1)S(1)}, bf16[2,4096,1024]{2,1,0:T(8,128)(2,1)}) %tuple.172), branch_computations={%region_6.0_spmd, %region_7.40_spmd} | conditional | flops 2235516672 | bytes 348985792 | solution.py:115
  318.0 20.9 %copy.11 = bf16[2,4096,1024]{1,2,0:T(8,128)(2,1)} copy(bf16[2,4096,1024]{2,1,0:T(8,128)(2,1)} %get-tuple-element.71) | data formatting | bytes 33554432 | tf_op jit(solution)/shard_map
  338.9 11.6 %fusion.206 = (bf16[2,256,1024]{1,2,0:T(8,128)(2,1)S(1)}, bf16[2,256,1024]{1,2,0:T(8,128)(2,1)S(1)}, bf16[2,256,1024]{1,2,0:T(8,128)(2,1)}, bf16[2,256,1024]{1,2...) fusion(bf16[2,4096,1024]{1,2,0:T(8,128)(2,1)} %copy.11), kind=kLoop, calls=%fused_computation.296 | loop fusion | bytes 33554432 | tf_op jit(solution)/shard_map/cond/branch_1_fun/slice | solution.py:109
  350.8 20.9 %copy.9 = bf16[2,4096,1024]{1,2,0:T(8,128)(2,1)} copy(bf16[2,4096,1024]{2,1,0:T(8,128)(2,1)} %get-tuple-element.69) | data formatting | bytes 33554432 | tf_op jit(solution)/shard_map
  371.7 7.2 %fusion.207 = (bf16[2,256,1024]{1,2,0:T(8,128)(2,1)S(1)}, bf16[2,256,1024]{1,2,0:T(8,128)(2,1)S(1)}, bf16[2,256,1024]{1,2,0:T(8,128)(2,1)S(1)}, bf16[2,256,1024]...) fusion(bf16[2,4096,1024]{1,2,0:T(8,128)(2,1)} %copy.9), kind=kLoop, calls=%fused_computation.297 | loop fusion | bytes 33554432 | tf_op jit(solution)/shard_map/cond/branch_1_fun/slice | solution.py:108
  387.0 1.5 fusion.12
  388.6 1.5 fusion.40
  391.6 1.7 fusion.32
  417.0 1.6 convolution_add_fusion
  418.6 2.3 conditional.8
  418.6 1.6 fusion.203
  420.8 6.3 %conditional.9 = (bf16[128,4096]{1,0:T(8,128)(2,1)S(1)}) conditional(s32[]{:T(128)} %convert_element_type.104, () %tuple.40, (bf16[128,1024]{1,0:T(8,128)(2,1)S(1)}, bf16[4096,1024]{1,0:T(8,128)(2,1)}) %tuple.48), branch_computations={%region_42.43_spmd, %region_43.44_spmd} | conditional | flops 1073741824 | bytes 9699336 | solution.py:129
  420.9 6.2 %fusion.208 = bf16[128,4096]{1,0:T(8,128)(2,1)S(1)} fusion(bf16[128,1024]{1,0:T(8,128)(2,1)S(1)} %get-tuple-element.58, bf16[4096,1024]{1,0:T(8,128)(2,1)} %get-tuple-element.59), kind=kOutput, calls=%fused_computation.298 | convolution fusion | flops 1073741824 | bytes 9699328 | tf_op jit(solution)/shard_map/cond/branch_1_fun/dot_general | solution.py:131
  428.1 31.8 %reduce-scatter.2.cloned.1.call-done = bf16[128,512]{1,0:T(8,128)(2,1)} async-done(((bf16[128,4096]{1,0:T(8,128)(2,1)}), bf16[128,512]{1,0:T(8,128)(2,1)}) %reduce-scatter.2.cloned.1.call-update) | async-done | bytes 131088 | tf_op jit(solution)/shard_map/reduce_scatter | solution.py:137
  460.0 1.7 add_convert_fusion
  (114 shorter events, 42.0 us)
Async XLA Ops:
  6.5 42.2 %all-gather.7.cloned.1.call-start = ((), (), s32[]{:S(2)}) async-start(), calls=%async_computation.2 | async-start | bytes 5242880 | tf_op jit(solution)/shard_map/all_gather | solution.py:56
  7.3 111.9 %all-gather.5.cloned.1.call-start = ((), (), s32[]{:S(2)}) async-start(), calls=%async_computation.1 | async-start | bytes 1310720 | tf_op jit(solution)/shard_map/all_gather | solution.py:57
  8.0 11.8 %copy-start.18 = (bf16[1,4096]{1,0:T(2,128)(2,1)S(1)}, bf16[1,4096]{1,0:T(2,128)(2,1)}, u32[]{:S(2)}) copy-start(bf16[1,4096]{1,0:T(2,128)(2,1)} %param.17) | copy-start | bytes 24580
  8.0 196.9 %all-gather.9.cloned.1.call-start = ((), (), s32[]{:S(2)}) async-start(), calls=%async_computation.3 | async-start | bytes 17825792 | tf_op jit(solution)/shard_map/all_gather | solution.py:98
  49.0 41.7 %collective-permute-start = (bf16[512,1024]{1,0:T(8,128)(2,1)S(1)}, bf16[512,1024]{1,0:T(8,128)(2,1)S(1)}, u32[]{:S(2)}, u32[]{:S(2)}) collective-permute-start(bf16[512,1024]{1,0:T(8,128)(2,1)S(1)} %get-tuple-element.62), channel_id=1, source_target_pairs={{0,64},{1,65},{2,66},{3,67},{4,68},{5,69},{6,70},{7,71},{8,72},{9,... | collective-permute-start | bytes 3145736 | tf_op jit(solution)/shard_map/ppermute | solution.py:16
  91.8 226.2 %all-gather.11.cloned.1.call-start = ((), (), s32[]{:S(2)}) async-start(), calls=%async_computation.4 | async-start | bytes 17825792 | tf_op jit(solution)/shard_map/all_gather | solution.py:99
  91.8 26.2 %collective-permute-start.1 = (bf16[512,1024]{1,0:T(8,128)(2,1)S(1)}, bf16[512,1024]{1,0:T(8,128)(2,1)S(1)}, u32[]{:S(2)}, u32[]{:S(2)}) collective-permute-start(bf16[512,1024]{1,0:T(8,128)(2,1)S(1)} %get-tuple-element.63), channel_id=1, source_target_pairs={{0,64},{1,65},{2,66},{3,67},{4,68},{5,69},{6,70},{7,71},{8,72},{9,... | collective-permute-start | bytes 3145736 | tf_op jit(solution)/shard_map/ppermute | solution.py:16
  118.0 1.0 copy-start.17
  119.0 340.9 %reduce-scatter.2.cloned.1.call-start = ((), (), s32[]{:S(2)}) async-start(), calls=%async_computation.5 | async-start | bytes 1179648 | tf_op jit(solution)/shard_map/reduce_scatter | solution.py:137
  119.1 198.8 %copy-start.19 = (s32[2]{0:T(128)S(1)}, s32[2]{0:T(128)}, u32[]{:S(2)}) copy-start(s32[2]{0:T(128)} %param.19) | copy-start | bytes 28
  397.8 1.6 copy-start.15
  399.4 1.2 copy-start.13
  400.6 1.2 copy-start.12
  401.9 1.2 copy-start.11
  403.1 1.2 copy-start.10
  404.3 1.2 copy-start.9
  405.5 1.2 copy-start.8
  406.8 1.2 copy-start.7
  408.0 1.2 copy-start.6
  409.2 1.2 copy-start.5
  410.4 1.2 copy-start.4
  411.7 1.2 copy-start.3
  412.9 1.2 copy-start.2
  414.1 1.2 copy-start.1
  (2 other events, 2.0 us)
Sparse Core Ops, SparseCore 0:
  9.0 39.6 all-gather.6
  50.4 20.1 all-gather.4
  91.9 112.9 all-gather.8
  206.9 111.0 all-gather.10
  428.2 31.6 reduce-scatter.1
where the time goes:
time: 472 us; the launch traced here: 468 us
  waiting for transfers between devices  319 us (68%)
  local copies, waits for them, and re-layouts  81.8 us (17%)
  matrix products  33.1 us (7%)
  other arithmetic  17.3 us (4%)
  between operations  13.2 us (3%)
    all_gather x1, waiting for transfers between devices, on_device(): value_part = lax.all_gather(value_flat, 'seq', axis=1, tiled=True)  113 us
    all_gather x1, waiting for transfers between devices, on_device(): key_part = lax.all_gather(key_flat, 'seq', axis=1, tiled=True)  78.8 us
    ppermute x2, waiting for transfers between devices, passed_along(): return lax.ppermute(shard, axis, pairs)  65.3 us
    another operation x4, local copies, waits for them, and re-layouts  42.1 us
    reduce_scatter x1, waiting for transfers between devices, on_device(): lax.psum_scatter(update_terms.astype(jnp.bfloat16), ('segment', 'mp'), sc...  31.8 us
    all_gather x1, waiting for transfers between devices, on_device(): lax.all_gather(memory.reshape(mem_count, part_width), 'mp', axis=1, tiled...  28.9 us
    dot_general x16, matrix products, fold_block(): jnp.einsum('bhqk,bkhd->bhqd', exp_scores.astype(jnp.bfloat16), value_head...  13.9 us
    reduce_sum x8, other arithmetic, fold_block(): totals = totals * rescale + jnp.sum(exp_scores, axis=-1)  12.2 us
  transfers between devices with their start and end apart: 7, of which 6 were waited for; matrix products, arithmetic and copies ran while one was open for 4% of the time, Pallas kernels for 0%

commit v1 on v0

v1 whole, which is shorter than its diff:
```python
import jax
import jax.numpy as jnp
from jax import lax
from jax.experimental import pallas as pl
from jax.experimental.pallas import tpu as pltpu
from jax.sharding import PartitionSpec as P

MESH = pl.DeviceIdType.MESH
EPS = 1e-6
MASKED = -1e30
SEQ = 16
GROUP = 8
ROWS = 256


def body(
    mem, dec, gain, w, lens, out,
    wbuf, xf, xd, xn, kvs, kvr, qs, qr, q2, acc, mx, tot, cs, cr, cx, rs, rr, res,
    w_sem, own_sem, ga_s, ga_r, gb_s, gb_r, gc_s, gc_r, kv_s, kv_r, q_s, q_r, c_s, c_r, rs_s, rs_r, res_s, res_r,
):
    s = lax.axis_index("segment")
    q = lax.axis_index("seq")
    m = lax.axis_index("mp")
    across = jnp.bitwise_xor(m, 2)
    beside = jnp.bitwise_xor(m, 1)
    corner = jnp.bitwise_xor(m, 3)
    rot = q // 2
    odd = q % 2
    group = jnp.where(s == 0, m, jnp.where(odd == 0, m, across))
    encoding = s == 0
    decoding = s == 1

    def remote(src, dst, ssem, rsem, device):
        return pltpu.make_async_remote_copy(
            src_ref=src, dst_ref=dst, send_sem=ssem, recv_sem=rsem, device_id=device, device_id_type=MESH
        )

    def kv_weight(j, t):
        return pltpu.make_async_copy(
            w.at[0, t, :, pl.ds(pl.multiple_of(j * 128, 128), 128)],
            wbuf.at[j, :, pl.ds(t * 128, 128)],
            w_sem.at[j, t],
        )

    def dec_weight(t, b):
        return pltpu.make_async_copy(
            w.at[0, t, :, pl.ds(b * 256, 256)], wbuf.at[4 * t + b], w_sem.at[4 * t + b, 0]
        )

    @pl.when(encoding)
    def _():
        for jj in range(8):
            for t in range(2):
                kv_weight(lax.rem(jj + rot, 8), t).start()

    @pl.when(decoding)
    def _():
        for t in range(2):
            for b in range(4):
                dec_weight(t, b).start()

    bar = pltpu.get_barrier_semaphore()

    def greet(k, _):
        for ss in range(2):
            for mm in (m, across):
                pl.semaphore_signal(bar, inc=1, device_id=(ss, k, mm), device_id_type=MESH)
        return 0

    lax.fori_loop(0, SEQ, greet, 0)
    for ss in range(2):
        for mm in (beside, corner):
            pl.semaphore_signal(bar, inc=1, device_id=(ss, q, mm), device_id_type=MESH)
    pl.semaphore_wait(bar, 4 * SEQ + 4)

    def mem_chunk(c):
        return mem.at[:, pl.ds(c * 128, 128), :]

    def own_mem(c):
        return pltpu.make_async_copy(mem_chunk(c), xf.at[m, c], own_sem.at[c])

    def a_mem(c):
        return remote(mem_chunk(c), xf.at[m, c], ga_s.at[c], ga_r.at[c], (0, q, across))

    def a_mem_in(c):
        return remote(mem_chunk(c), xf.at[across, c], ga_s.at[c], ga_r.at[c], (0, q, across))

    def b_mem(c):
        return remote(mem_chunk(c), xf.at[m, c], gb_s.at[c], gb_r.at[c], (0, q, beside))

    def c_mem(c):
        return remote(xf.at[across, c], xf.at[across, c], gc_s.at[c], gc_r.at[c], (0, q, beside))

    own_dec = pltpu.make_async_copy(dec, xd.at[m], own_sem.at[0])
    a_dec = remote(dec, xd.at[m], ga_s.at[0], ga_r.at[0], (1, q, across))
    b_dec = remote(dec, xd.at[m], gb_s.at[0], gb_r.at[0], (1, q, beside))
    c_dec = remote(xd.at[across], xd.at[across], gc_s.at[0], gc_r.at[0], (1, q, beside))

    def normalise(load, rows):
        def step(r, _):
            start = pl.multiple_of(r * 16, 16)
            total = jnp.zeros((16, 1), jnp.float32)
            for k in range(4):
                part = load(k, start).astype(jnp.float32)
                total = total + jnp.sum(part * part, axis=1, keepdims=True)
            inverse = lax.rsqrt(total * (1.0 / 4096) + EPS)
            for k in range(4):
                part = load(k, start).astype(jnp.float32)
                wide = part * inverse * gain[:, k * 1024 : (k + 1) * 1024].astype(jnp.float32)
                xn[pl.ds(start, 16), k * 1024 : (k + 1) * 1024] = wide.astype(jnp.bfloat16)
            return 0

        lax.fori_loop(0, rows // 16, step, 0)

    low = lax.broadcasted_iota(jnp.int32, (1, 128), 1) < 64

    def kv_out(c, i, doc, device):
        return remote(kvs.at[c, i, doc], kvr.at[c, q], kv_s.at[c, i, doc], kv_r.at[c, q], device)

    def unit_of(doc, i, e):
        return (0, i, m) if doc == 0 else (1, i, m if e == 0 else across)

    @pl.when(encoding)
    def _():
        a_dec.start()
        for c in range(2):
            own_mem(c).start()
            b_mem(c).start()
        for c in range(2):
            a_mem_in(c).wait_recv()
            c_mem(c).start()
            own_mem(c).wait()
            b_mem(c).wait_recv()
            c_mem(c).wait_recv()

            def load(k, start, c=c):
                return xf[k, c, start // 128, pl.ds(pl.multiple_of(start % 128, 16), 16), :]

            normalise(load, 256)

            def project(jj, _, c=c):
                j = lax.rem(jj + rot, 8)
                if c == 0:
                    for t in range(2):
                        kv_weight(j, t).wait()
                both = jnp.dot(xn[...], wbuf[j], preferred_element_type=jnp.float32)
                key, value = both[:, :128], both[:, 128:]
                key = pltpu.roll(key, 64, 1)
                for e in range(2):
                    i = 2 * j + e
                    tile = jnp.where(low, value, key) if e == 0 else jnp.where(low, key, value)
                    tile = tile.astype(jnp.bfloat16).reshape(2, 128, 128)
                    kvs[c, i] = tile

                    @pl.when(i == q)
                    def _(tile=tile):
                        kvr[c, q] = tile[0]

                    kv_out(c, i, 1, unit_of(1, i, e)).start()

                    @pl.when(i != q)
                    def _(i=i, e=e):
                        kv_out(c, i, 0, unit_of(0, i, e)).start()

                return 0

            lax.fori_loop(0, 8, project, 0)

    def q_out(i, doc, device):
        return remote(
            qs.at[i // 2, doc], qr.at[q], q_s.at[i, doc], q_r.at[q], device
        )

    residual_out = remote(
        xd.at[m // 2, :, :, pl.ds(pl.multiple_of((m % 2) * 512, 512), 512)], res, res_s, res_r, (0, q, m)
    )

    @pl.when(decoding)
    def _():
        for c in range(2):
            a_mem(c).start()
        own_dec.start()
        b_dec.start()
        remote(dec, xd.at[across], ga_s.at[0], ga_r.at[0], (1, q, across)).wait_recv()
        c_dec.start()
        own_dec.wait()
        b_dec.wait_recv()
        c_dec.wait_recv()
        residual_out.start()

        def load(k, start):
            return xd[k, start // 64, pl.ds(pl.multiple_of(start % 64, 16), 16), :]

        normalise(load, 128)
        for b in range(4):
            dec_weight(0, b).wait()
            made = jnp.dot(xn[:128, :], wbuf[b], preferred_element_type=jnp.float32)
            for u in range(2):
                t = 2 * b + u
                tile = pltpu.roll(made[:, u * 128 : (u + 1) * 128], 64, 1)
                tile = tile.astype(jnp.bfloat16).reshape(2, 64, 128)
                qs[t] = tile
                for e in range(2):
                    i = 2 * t + e
                    q_out(i, 0, unit_of(0, i, e)).start()
                    if e == 1:
                        q_out(i, 1, unit_of(1, i, e)).start()
                    else:

                        @pl.when(q != i)
                        def _(i=i, e=e):
                            q_out(i, 1, unit_of(1, i, e)).start()

                        @pl.when(q == i)
                        def _(tile=tile):
                            qr[q] = tile[1]

    def q_in(k, _):
        @pl.when(jnp.logical_or(encoding, jnp.logical_or(odd == 1, k != q)))
        def _():
            remote(qs.at[0, 0], qr.at[k], q_s.at[0, 0], q_r.at[k], (s, q, m)).wait_recv()

        return 0

    lax.fori_loop(0, SEQ, q_in, 0)
    lane = lax.broadcasted_iota(jnp.int32, (1, 128), 1)
    key_half = jnp.where(odd == 1, 0, 1)
    key_lane = (lane // 64) == key_half
    q2[...] = jnp.where(key_lane, qr[...].reshape(1024, 128), jnp.bfloat16(0))
    mx[...] = jnp.full_like(mx, MASKED)
    tot[...] = jnp.zeros_like(tot)
    acc[...] = jnp.zeros_like(acc)
    length = lens[s]
    span = GROUP * 128

    def attend(step, _):
        c = step // (SEQ // GROUP)
        g = step % (SEQ // GROUP)

        def kv_in(k, _):
            src = g * GROUP + k

            @pl.when(jnp.logical_or(decoding, src != q))
            def _():
                remote(kvs.at[0, 0, 0], kvr.at[c, src], kv_s.at[0, 0, 0], kv_r.at[c, src], (s, q, m)).wait_recv()

            return 0

        lax.fori_loop(0, GROUP, kv_in, 0)
        kv = kvr[c, pl.ds(g * GROUP, GROUP)].reshape(span, 128)
        col = lax.broadcasted_iota(jnp.int32, (1, span), 1)
        position = (g * GROUP + col // 128) * 256 + c * 128 + col % 128
        valid = position < length
        for r in range(1024 // ROWS):
            rows = pl.ds(r * ROWS, ROWS)
            scores = lax.dot_general(
                q2[rows, :], kv, (((1,), (1,)), ((), ())), preferred_element_type=jnp.float32
            )
            scores = jnp.where(valid, scores, MASKED)
            before = mx[rows, :]
            after = jnp.maximum(before, jnp.max(scores, axis=1, keepdims=True))
            probs = jnp.exp(scores - jnp.concatenate([after] * GROUP, axis=1))
            scale = jnp.exp(before - after)
            part = probs[:, :128]
            for k in range(1, GROUP):
                part = part + probs[:, k * 128 : (k + 1) * 128]
            tot[rows, :] = tot[rows, :] * scale + part
            acc[rows, :] = acc[rows, :] * scale + jnp.dot(
                probs.astype(jnp.bfloat16), kv, preferred_element_type=jnp.float32
            )
            mx[rows, :] = after
        return 0

    lax.fori_loop(0, 2 * SEQ // GROUP, attend, 0)

    def c_out(k):
        return remote(cs.at[k], cr.at[s, q], c_s.at[k], c_r.at[s, q], (1, k, group))

    own_context = jnp.logical_and(decoding, odd == 0)

    for k in range(SEQ):
        rows = pl.ds(k * 64, 64)
        total = jnp.sum(tot[rows, :], axis=1, keepdims=True)
        context = jnp.where(key_lane, 0.0, acc[rows, :] / total).astype(jnp.bfloat16)
        cs[k] = context
        mine = jnp.logical_and(own_context, q == k)

        @pl.when(mine)
        def _(context=context):
            cr[1, q] = context

        @pl.when(jnp.logical_not(mine))
        def _(k=k):
            c_out(k).start()

    def rs_out(g):
        return remote(rs.at[g], rr.at[m], rs_s.at[g], rs_r.at[m], (g // 4, q, g % 4))

    @pl.when(decoding)
    def _():
        def c_in(k, _):
            remote(cs.at[0], cr.at[0, k], c_s.at[0], c_r.at[0, k], (s, q, m)).wait_recv()

            @pl.when(jnp.logical_or(odd == 1, k != q))
            def _():
                remote(cs.at[0], cr.at[1, k], c_s.at[0], c_r.at[1, k], (s, q, m)).wait_recv()

            return 0

        lax.fori_loop(0, SEQ, c_in, 0)
        for d in range(2):
            for t in range(8):
                cx[d * 64 : (d + 1) * 64, t * 128 : (t + 1) * 128] = cr[d, 2 * t] + cr[d, 2 * t + 1]
        for b in range(4):
            dec_weight(1, b).wait()

        for g in range(8):
            part = jnp.zeros((128, 512), jnp.float32)
            for b in range(4):
                part = part + lax.dot_general(
                    cx[:, b * 256 : (b + 1) * 256],
                    wbuf[4 + b, g * 512 : (g + 1) * 512, :],
                    (((1,), (1,)), ((), ())),
                    preferred_element_type=jnp.float32,
                )
            rs[g] = part.astype(jnp.bfloat16).reshape(2, 64, 512)
            if g < 4:
                rs_out(g).start()
            else:

                @pl.when(m != g - 4)
                def _(g=g):
                    rs_out(g).start()

                @pl.when(m == g - 4)
                def _(part=part):
                    rr[m] = part.astype(jnp.bfloat16).reshape(2, 64, 512)
                    res[...] = xd[2 + m // 2, :, :, pl.ds(pl.multiple_of((m % 2) * 512, 512), 512)]

    @pl.when(encoding)
    def _():
        residual_out.wait_recv()

    for k in range(4):

        @pl.when(jnp.logical_or(encoding, m != k))
        def _(k=k):
            remote(rs.at[0], rr.at[k], rs_s.at[0], rs_r.at[k], (s, q, m)).wait_recv()

    update = rr[0].astype(jnp.float32)
    for k in range(1, 4):
        update = update + rr[k].astype(jnp.float32)
    out[...] = (res[...].astype(jnp.float32) + update).astype(jnp.bfloat16)

    def c_done(k, _):
        @pl.when(jnp.logical_not(jnp.logical_and(own_context, q == k)))
        def _():
            c_out(k).wait_send()

        return 0

    lax.fori_loop(0, SEQ, c_done, 0)

    @pl.when(encoding)
    def _():
        a_dec.wait_send()
        for c in range(2):
            b_mem(c).wait_send()
            c_mem(c).wait_send()

        def kv_done(i, _):
            for c in range(2):
                kv_out(c, i, 1, (1, q, m)).wait_send()

                @pl.when(i != q)
                def _(c=c):
                    kv_out(c, i, 0, (1, q, m)).wait_send()

            return 0

        lax.fori_loop(0, SEQ, kv_done, 0)

    @pl.when(decoding)
    def _():
        for c in range(2):
            a_mem(c).wait_send()
        b_dec.wait_send()
        c_dec.wait_send()
        residual_out.wait_send()

        def q_done(i, _):
            q_out(i, 0, (0, q, m)).wait_send()

            @pl.when(jnp.logical_or(odd == 1, i != q))
            def _():
                q_out(i, 1, (0, q, m)).wait_send()

            return 0

        lax.fori_loop(0, SEQ, q_done, 0)
        for g in range(8):

            @pl.when(m != g - 4)
            def _(g=g):
                rs_out(g).wait_send()


def on_device(memory, decoder_rows, gains, weights, lengths):
    bf16, f32 = jnp.bfloat16, jnp.float32
    anywhere = pl.BlockSpec(memory_space=pl.ANY)
    vmem = pl.BlockSpec(memory_space=pltpu.VMEM)
    dma = pltpu.SemaphoreType.DMA
    return pl.pallas_call(
        body,
        name="cross_attention",
        out_shape=jax.ShapeDtypeStruct((2, 64, 512), bf16),
        in_specs=[anywhere, anywhere, vmem, anywhere, pl.BlockSpec(memory_space=pltpu.SMEM)],
        out_specs=vmem,
        scratch_shapes=[
            pltpu.VMEM((8, 4096, 256), bf16),
            pltpu.VMEM((4, 2, 2, 128, 1024), bf16),
            pltpu.VMEM((4, 2, 64, 1024), bf16),
            pltpu.VMEM((256, 4096), bf16),
            pltpu.VMEM((2, 16, 2, 128, 128), bf16),
            pltpu.VMEM((2, 16, 128, 128), bf16),
            pltpu.VMEM((8, 2, 64, 128), bf16),
            pltpu.VMEM((16, 64, 128), bf16),
            pltpu.VMEM((1024, 128), bf16),
            pltpu.VMEM((1024, 128), f32),
            pltpu.VMEM((1024, 128), f32),
            pltpu.VMEM((1024, 128), f32),
            pltpu.VMEM((16, 64, 128), bf16),
            pltpu.VMEM((2, 16, 64, 128), bf16),
            pltpu.VMEM((128, 1024), bf16),
            pltpu.VMEM((8, 2, 64, 512), bf16),
            pltpu.VMEM((4, 2, 64, 512), bf16),
            pltpu.VMEM((2, 64, 512), bf16),
            dma((8, 2)),
            dma((2,)),
            dma((2,)),
            dma((2,)),
            dma((2,)),
            dma((2,)),
            dma((2,)),
            dma((2,)),
            dma((2, 16, 2)),
            dma((2, 16)),
            dma((16, 2)),
            dma((16,)),
            dma((16,)),
            dma((2, 16)),
            dma((8,)),
            dma((4,)),
            dma,
            dma,
        ],
        compiler_params=pltpu.CompilerParams(
            collective_id=0, has_side_effects=True, vmem_limit_bytes=56 << 20
        ),
    )(memory, decoder_rows, gains, weights, lengths)


def solution(mesh):
    in_specs = (
        P(None, "seq", "mp"),
        P(None, "seq", "mp"),
        P("segment", None),
        P("segment", None, None, "mp"),
        P(),
    )
    out_specs = P(None, "seq", ("segment", "mp"))
    return jax.shard_map(
        on_device, mesh=mesh, in_specs=in_specs, out_specs=out_specs, check_vma=False
    )
```

time: 472 us -> 79.9 us (0.17)
  waiting for transfers between devices: 319 us -> 0 us
  local copies, waits for them, and re-layouts: 81.8 us -> 1.57 us
  Pallas kernels: 0 us -> 77.7 us
  matrix products: 33.1 us -> 0 us
  other arithmetic: 17.3 us -> 0 us
  between operations: 13.2 us -> 0.01 us
    all_gather x4 -> x0, waiting for transfers between devices: 221 us -> none  [the longest x1 113 us: on_device(): value_part = lax.all_gather(value_flat, 'seq', axis=1, tiled=True)]
    pallas_call x0 -> x1, Pallas kernels: none -> 77.7 us  [on_device(): pl.pallas_call(body, name='cross_attention', out_shape=jax.ShapeDtypeStru...]
    ppermute x2 -> x0, waiting for transfers between devices: 65.3 us -> none  [passed_along(): return lax.ppermute(shard, axis, pairs)]
    another operation x4 -> x0, local copies, waits for them, and re-layouts: 42.1 us -> none
    dot_general x34 -> x0, matrix products: 33.1 us -> none  [the longest x16 13.9 us: fold_block(): jnp.einsum('bhqk,bkhd->bhqd', exp_scores.astype(jnp.bfloat16), value_head...]
    reduce_scatter x1 -> x0, waiting for transfers between devices: 31.8 us -> none  [on_device(): lax.psum_scatter(update_terms.astype(jnp.bfloat16), ('segment', 'mp'), sc...]
    slice x2 -> x0, local copies, waits for them, and re-layouts: 18.8 us -> none  [the longest x1 11.6 us: attend(): value_part[:, offset:offset + width]]
    reduce_sum x9 -> x0, other arithmetic: 13.7 us -> none  [the longest x8 12.2 us: fold_block(): totals = totals * rescale + jnp.sum(exp_scores, axis=-1)]
  transfers between devices with their start and end apart: 7 -> 0, of which waited for: 6 -> 0; matrix products, arithmetic and copies ran while one was open for 4% -> 0% of each run, Pallas kernels for 0% -> 0%
where the time goes in v1:
time: 79.9 us; the launch traced here: 79.3 us
  Pallas kernels  77.7 us (97%)
  local copies, waits for them, and re-layouts  1.57 us (2%)
    pallas_call x1, Pallas kernels, on_device(): pl.pallas_call(body, name='cross_attention', out_shape=jax.ShapeDtypeStru...  77.7 us

profile of v1, /device:TPU:7, one launch (start us, length us, event | category | flops | bytes accessed | tf_op | source)
XLA Modules:
  0.0 79.3 jit_solution(3841520923480628489)
XLA Ops:
  0.0 77.7 %cross_attention.1 = bf16[2,64,512]{2,1,0:T(8,128)(2,1)} custom-call(bf16[2,256,1024]{2,1,0:T(8,128)(2,1)} %mem.1, bf16[2,64,1024]{2,1,0:T(8,128)(2,1)} %dec.1, bf16[1,4096]{1,0:T(2,128)(2,1)} %gain.1, bf16[1,2,4096,1024]{3,2,1,0:T(8,128)(2,1)} %w.1, s32[2]{0:T(128)} %lens.1), custom_call_target="tpu_custom_call" | custom-call | tf_op jit(solution)/shard_map/cross_attention/pallas_call | solution.py:413
  77.7 1.6 %copy.7 = bf16[2,64,512]{2,1,0:T(8,128)(2,1)} copy(bf16[2,64,512]{2,1,0:T(8,128)(2,1)} %cross_attention.1) | data formatting | bytes 262144

commit v2 on v0

v2 whole, which is shorter than its diff:
```python
import jax
import jax.numpy as jnp
from jax import lax
from jax.experimental import pallas as pl
from jax.experimental.pallas import tpu as pltpu
from jax.sharding import PartitionSpec as P

MESH = pl.DeviceIdType.MESH
EPS = 1e-6
MASKED = -1e30
SEQ = 16
ROWS = 256
SPAN = 2048
PIECE = 16
DIRECT = ((0, 1, 2, 3, 4), (8, 9, 10, 11, 12))
RELAYED = (5, 6, 7, 13, 14, 15)
ARRIVAL = ((0, 1, 2, 5, 3, 6, 4, 7), (8, 9, 10, 13, 11, 14, 12, 15))


def seq_of(n):
    return (n % 4) * 4 + (n // 4 + n % 4) % 4


def body(
    mem, dec, gain, w, lens, out,
    wbuf, wo, xf, xd, relay, xn, kvs, kvr, qs, qr, q2, acc, mx, cs, cr, cx, rs, rr, res,
    w_sem, wo_sem, wx_s, wx_r, own_sem, gp_r, gf_r, fl_s, fw_s, gb_s, gb_r, d_s, d_r,
    kv_s, kv_r, q_s, q_r, c_s, c_r, x_s, x_r, rs_s, rs_r, res_s, res_r,
):
    s = lax.axis_index("segment")
    q = lax.axis_index("seq")
    m = lax.axis_index("mp")
    across = jnp.bitwise_xor(m, 2)
    beside = jnp.bitwise_xor(m, 1)
    half, core = m // 2, m % 2
    z, y = q // 4, q % 4
    slot = 4 * lax.rem(y - z + 4, 4) + z
    odd = z % 2
    group = jnp.where(s == 0, m, jnp.where(odd == 0, m, across))
    encoding = s == 0
    decoding = s == 1

    def remote(src, dst, ssem, rsem, device):
        return pltpu.make_async_remote_copy(
            src_ref=src, dst_ref=dst, send_sem=ssem, recv_sem=rsem, device_id=device, device_id_type=MESH
        )

    def kv_weight(j, t):
        return pltpu.make_async_copy(
            w.at[0, t, :, pl.ds(pl.multiple_of(j * 256, 256), 256)],
            wbuf.at[j, :, pl.ds(t * 256, 256)],
            w_sem,
        )

    def q_weight(b):
        return pltpu.make_async_copy(w.at[0, 0, :, pl.ds(b * 512, 512)], wbuf.at[b], w_sem)

    def out_rows(k, c):
        return w.at[0, 1, pl.ds(pl.multiple_of((2 * k + c) * 512, 512), 512), :]

    def o_weight(k):
        return pltpu.make_async_copy(out_rows(k, core), wo.at[core, k], wo_sem)

    def o_weight_out(k):
        return remote(out_rows(k, 1 - core), wo.at[core, k], wx_s, wx_r, (1, q, beside))

    @pl.when(encoding)
    def _():
        for jj in range(4):
            for t in range(2):
                kv_weight(jj, t).start()

    @pl.when(decoding)
    def _():
        for b in range(2):
            q_weight(b).start()
        for k in range(4):
            o_weight(k).start()

    bar = pltpu.get_barrier_semaphore()

    def hello(*device):
        pl.semaphore_signal(bar, inc=1, device_id=device, device_id_type=MESH)

    def greet(k, _):
        k_odd = (k // 4) % 2 == 1
        hello(0, k, m)

        @pl.when(jnp.logical_or(encoding, jnp.logical_not(jnp.logical_and(k_odd, odd == 1))))
        def _():
            hello(1, k, m)

        @pl.when(jnp.logical_or(k_odd, jnp.logical_and(decoding, jnp.logical_or(odd == 1, k == q))))
        def _():
            hello(1, k, across)

        @pl.when(jnp.logical_and(decoding, jnp.logical_or(odd == 1, k == q)))
        def _():
            hello(0, k, across)

        @pl.when(jnp.logical_and(encoding, jnp.logical_and(odd == 0, k == q)))
        def _():
            hello(1, k, across)

        return 0

    hello(s, q, beside)
    lax.fori_loop(0, SEQ, greet, 0)
    peers = jnp.where(encoding, jnp.where(odd == 1, 41, 42), jnp.where(odd == 1, 57, 43))
    pl.semaphore_wait(bar, peers)

    def piece(ref, p):
        return ref.at[:, pl.ds(p * PIECE, PIECE), :]

    def direct(p):
        return remote(piece(mem, p), piece(xf.at[m], p), fl_s, gp_r.at[p], (0, q, across))

    def hop(n):
        p = RELAYED[n]
        return remote(piece(mem, p), relay.at[n], fl_s, gp_r.at[p], (1, q, across))

    def relayed(n):
        p = RELAYED[n]
        return remote(relay.at[n], piece(xf.at[across], p), fw_s, gp_r.at[p], (0, q, m))

    def piece_in(p):
        return remote(piece(mem, p), piece(xf.at[across], p), fl_s, gp_r.at[p], (0, q, m))

    def forward(p):
        return remote(
            piece(xf.at[across], p), piece(xf.at[across], p), fw_s, gf_r.at[p], (0, q, beside)
        )

    def forward_in(p):
        there = jnp.bitwise_xor(beside, 2)
        return remote(piece(mem, p), piece(xf.at[there], p), fw_s, gf_r.at[p], (0, q, beside))

    def mem_half(c):
        return mem.at[:, pl.ds(c * 128, 128), :]

    own_mem = pltpu.make_async_copy(mem, xf.at[m], own_sem)

    def b_mem(c):
        return remote(
            mem_half(c), xf.at[m, :, pl.ds(c * 128, 128), :], gb_s.at[c], gb_r.at[c], (0, q, beside)
        )

    own_dec = pltpu.make_async_copy(dec, xd.at[m], own_sem)
    a_dec = remote(dec, xd.at[m], d_s.at[0], d_r.at[0], (1, q, across))
    b_dec = remote(dec, xd.at[m], d_s.at[0], d_r.at[1], (1, q, beside))
    c_dec = remote(xd.at[across], xd.at[across], d_s.at[1], d_r.at[2], (1, q, beside))

    def normalise(source, start, put):
        total = jnp.zeros((2, PIECE, 1), jnp.float32)
        for k in range(4):
            part = source[k, :, pl.ds(start, PIECE), :].astype(jnp.float32)
            total = total + jnp.sum(part * part, axis=2, keepdims=True)
        inverse = lax.rsqrt(total * (1.0 / 4096) + EPS)
        for k in range(4):
            part = source[k, :, pl.ds(start, PIECE), :].astype(jnp.float32)
            wide = part * inverse * gain[:, k * 1024 : (k + 1) * 1024].astype(jnp.float32)
            put(slice(k * 1024, (k + 1) * 1024), wide.astype(jnp.bfloat16))

    low = lax.broadcasted_iota(jnp.int32, (1, 128), 1) < 64

    def tile_of(c, i, doc):
        return (c * SEQ + i) * 2 + doc

    def kv_out(c, i, doc, device):
        return remote(kvs.at[tile_of(c, i, doc)], kvr.at[c, q], kv_s, kv_r.at[c], device)

    def unit_of(doc, i, e):
        return (0, seq_of(i), m) if doc == 0 else (1, seq_of(i), m if e % 2 == 0 else across)

    def normalise_mem(p):
        c, at = p // 8, (p % 8) * PIECE

        def put(columns, value):
            xn[c, at : at + PIECE, columns] = value[0]
            xn[c, 128 + at : 128 + at + PIECE, columns] = value[1]

        normalise(xf, p * PIECE, put)

    @pl.when(encoding)
    def _():
        hop(0).start()
        b_mem(0).start()
        for n in range(1, 6):
            hop(n).start()
        a_dec.start()
        own_mem.start()

        def ready(p):
            forward_in(p).wait_recv()
            normalise_mem(p)

        own_mem.wait()
        b_mem(0).wait_recv()
        for n, p in enumerate(ARRIVAL[0]):
            piece_in(p).wait_recv()
            forward(p).start()
            if n >= 2:
                ready(ARRIVAL[0][n - 2])
        b_mem(1).start()
        ready(ARRIVAL[0][6])
        ready(ARRIVAL[0][7])
        pltpu.make_async_copy(wbuf, wbuf, w_sem).wait()

        def project(c, jj):
            j = lax.rem(jj + y, 4)
            both = jnp.dot(xn[c], wbuf[j], preferred_element_type=jnp.float32)
            for u in range(2):
                key = pltpu.roll(both[:, u * 128 : (u + 1) * 128], 64, 1)
                value = both[:, 256 + u * 128 : 256 + (u + 1) * 128]
                for e in range(2):
                    i = 4 * j + 2 * u + e
                    tile = jnp.where(low, value, key) if e == 0 else jnp.where(low, key, value)
                    kvs[pl.ds(tile_of(c, i, 0), 2)] = tile.astype(jnp.bfloat16).reshape(2, 128, 128)
            for e in range(4):
                i = 4 * j + e
                kv_out(c, i, 1, unit_of(1, i, e)).start()

                @pl.when(i != slot)
                def _(i=i, e=e):
                    kv_out(c, i, 0, unit_of(0, i, e)).start()

                @pl.when(i == slot)
                def _(i=i):
                    pltpu.make_async_copy(kvs.at[tile_of(c, i, 0)], kvr.at[c, q], kv_r.at[c]).start()

        waiting = []
        for jj in range(4):
            project(0, jj)
            for p in waiting:
                ready(p)
            waiting = ARRIVAL[1][2 * jj : 2 * jj + 2]
            if jj == 0:
                b_mem(1).wait_recv()
            for p in waiting:
                piece_in(p).wait_recv()
                forward(p).start()
        for p in waiting:
            ready(p)
        for jj in range(4):
            project(1, jj)

    def q_out(i, doc, device):
        return remote(qs.at[i, doc], qr.at[slot], q_s, q_r, device)

    residual_out = remote(
        xd.at[m // 2, :, :, pl.ds(pl.multiple_of((m % 2) * 512, 512), 512)], res, res_s, res_r, (0, q, m)
    )

    @pl.when(decoding)
    def _():
        for p in DIRECT[0]:
            direct(p).start()
        own_dec.start()
        b_dec.start()

        def pass_on(n):
            p = RELAYED[n]
            remote(piece(mem, p), relay.at[n], fl_s, gp_r.at[p], (1, q, across)).wait_recv()
            relayed(n).start()

        for n in range(3):
            pass_on(n)
        for p in DIRECT[1]:
            direct(p).start()
        for n in range(3, 6):
            pass_on(n)
        remote(dec, xd.at[across], d_s.at[0], d_r.at[0], (1, q, across)).wait_recv()
        c_dec.start()
        own_dec.wait()
        b_dec.wait_recv()
        c_dec.wait_recv()
        for p in range(4):

            def put(columns, value, p=p):
                xn[0, p * PIECE : (p + 1) * PIECE, columns] = value[0]
                xn[0, 64 + p * PIECE : 64 + (p + 1) * PIECE, columns] = value[1]

            normalise(xd, p * PIECE, put)
        pltpu.make_async_copy(wbuf.at[0:2], wbuf.at[0:2], w_sem).wait()
        for b in range(2):
            made = jnp.dot(xn[0, :128, :], wbuf[b], preferred_element_type=jnp.float32)
            for u in range(4):
                pair = made[:, u * 128 : (u + 1) * 128]
                turned = pltpu.roll(pair, 64, 1)
                pair, turned = (v.reshape(2, 2, 32, 128) for v in (pair, turned))
                for e in range(2):
                    first, second = (pair, turned) if e == 0 else (turned, pair)
                    tile = jnp.where(low, first[:, 0], second[:, 1])
                    qs[2 * (4 * b + u) + e] = tile.astype(jnp.bfloat16)
            for i in range(8 * b, 8 * b + 8):
                q_out(i, 0, unit_of(0, i, i)).start()
                if i % 2 == 1:
                    q_out(i, 1, unit_of(1, i, i)).start()
                else:

                    @pl.when(slot != i)
                    def _(i=i):
                        q_out(i, 1, unit_of(1, i, i)).start()

                    @pl.when(slot == i)
                    def _(i=i):
                        pltpu.make_async_copy(qs.at[i, 1], qr.at[slot], q_r).start()
        residual_out.start()
        for k in range(4):
            o_weight_out(k).start()

    pltpu.make_async_copy(qr, qr, q_r).wait()
    lane = lax.broadcasted_iota(jnp.int32, (1, 128), 1)
    key_half = jnp.where(odd == 1, 0, 1)
    key_lane = (lane // 64) == key_half
    packed = qr[...].astype(jnp.float32)
    turned = pltpu.roll(packed, 64, 2)
    first = jnp.where(odd == 1, packed, turned)
    second = jnp.where(odd == 1, turned, packed)
    placed = jnp.stack([first, second], axis=1).reshape(1024, 128)
    q2[...] = jnp.where(key_lane, placed, 0.0).astype(jnp.bfloat16)
    length = lens[s]
    one = jnp.bfloat16(1)
    column = lax.broadcasted_iota(jnp.int32, (1, SPAN), 1)
    within = (column // 128) * 256 + column % 128

    def kv_wait(c):
        pltpu.make_async_copy(kvr.at[c], kvr.at[c], kv_r.at[c]).wait()

    def score(c, rows):
        return lax.dot_general(
            q2[rows, :],
            kvr[c].reshape(SPAN, 128),
            (((1,), (1,)), ((), ())),
            preferred_element_type=jnp.float32,
        )

    def weigh(c, scores, before):
        scores = jnp.where(within + c * 128 < length, scores, MASKED)
        top = jnp.max(scores, axis=1, keepdims=True)
        top = jnp.broadcast_to(top, (ROWS, 128)) if before is None else jnp.maximum(before, top)
        probs = jnp.exp(scores - jnp.concatenate([top] * (SPAN // 128), axis=1)).astype(jnp.bfloat16)
        mixed = jnp.dot(
            probs,
            jnp.where(key_lane, one, kvr[c].reshape(SPAN, 128)),
            preferred_element_type=jnp.float32,
        )
        return top, mixed

    def block(r):
        return pl.ds(pl.multiple_of(r * ROWS, ROWS), ROWS)

    blocks = 1024 // ROWS
    kv_wait(0)
    scores = score(0, block(0))
    for r in range(blocks):
        following = score(0, block(r + 1)) if r + 1 < blocks else None
        top, mixed = weigh(0, scores, None)
        mx[block(r), :] = top
        acc[block(r), :] = mixed
        scores = following

    def c_out(k):
        return remote(cs.at[k], cr.at[s, slot], c_s, c_r, (1, seq_of(k), group))

    own_context = jnp.logical_and(decoding, odd == 0)

    kv_wait(1)
    order = [lax.rem(r + y, blocks) for r in range(blocks)]
    scores = score(1, block(order[0]))
    for n, r in enumerate(order):
        following = score(1, block(order[n + 1])) if n + 1 < blocks else None
        before = mx[block(r), :]
        top, mixed = weigh(1, scores, before)
        mixed = acc[block(r), :] * jnp.exp(before - top) + mixed
        context = mixed / pltpu.roll(mixed, 64, 1)
        context = jnp.where(key_lane, pltpu.roll(context, 64, 1), context).reshape(4, 2, 32, 128)
        cs[pl.ds(r * 4, 4)] = jnp.where(low, context[:, 0], context[:, 1]).astype(jnp.bfloat16)
        for k in range(4):
            to = r * 4 + k
            mine = jnp.logical_and(own_context, slot == to)

            @pl.when(mine)
            def _():
                pltpu.make_async_copy(cs.at[slot], cr.at[1, slot], c_r).start()

            @pl.when(jnp.logical_not(mine))
            def _(to=to):
                c_out(to).start()

        scores = following

    def x_out(c):
        return remote(cx.at[c], cx.at[c], x_s, x_r, (1, q, beside))

    def rs_out(k):
        return remote(rs.at[k], rr.at[half], rs_s, rs_r, (k // 2, q, 2 * (k % 2) + core))

    @pl.when(decoding)
    def _():
        pltpu.make_async_copy(cr, cr, c_r).wait()
        for d in range(2):
            for t in range(8):
                first = cr[d, 2 * t].astype(jnp.float32)
                second = cr[d, 2 * t + 1].astype(jnp.float32)
                at = slice(t * 128, (t + 1) * 128)
                upper = jnp.where(low, first, pltpu.roll(second, 64, 1))
                lower = jnp.where(low, pltpu.roll(first, 64, 1), second)
                cx[core, d * 64 : d * 64 + 32, at] = upper.astype(jnp.bfloat16)
                cx[core, d * 64 + 32 : d * 64 + 64, at] = lower.astype(jnp.bfloat16)
        x_out(core).start()
        pltpu.make_async_copy(wo.at[core], wo.at[core], wo_sem).wait()
        remote(wo.at[core], wo.at[1 - core], wx_s, wx_r, (1, q, beside)).wait_recv()

        def partial(c, k):
            return lax.dot_general(
                cx[c], wo[c, k], (((1,), (1,)), ((), ())), preferred_element_type=jnp.float32
            )

        far, own = 3 - half, 2 + half
        part = partial(core, far)
        x_out(1 - core).wait_recv()
        part = part + partial(1 - core, far)
        rs[far] = part.astype(jnp.bfloat16).reshape(2, 64, 512)
        rs_out(far).start()
        for k in range(2):
            part = partial(0, k) + partial(1, k)
            rs[k] = part.astype(jnp.bfloat16).reshape(2, 64, 512)
            rs_out(k).start()
        part = partial(0, own) + partial(1, own)
        rr[half] = part.astype(jnp.bfloat16).reshape(2, 64, 512)
        res[...] = xd[2 + half, :, :, pl.ds(pl.multiple_of(core * 512, 512), 512)]

    @pl.when(encoding)
    def _():
        residual_out.wait_recv()

    @pl.when(encoding)
    def _():
        pltpu.make_async_copy(rr, rr, rs_r).wait()

    @pl.when(decoding)
    def _():
        pltpu.make_async_copy(rr.at[0], rr.at[0], rs_r).wait()

    update = rr[0].astype(jnp.float32) + rr[1].astype(jnp.float32)
    out[...] = (res[...].astype(jnp.float32) + update).astype(jnp.bfloat16)

    def sent(ref, sem):
        remote(ref, ref, sem, sem, (s, q, m)).wait_send()

    @pl.when(jnp.logical_not(own_context))
    def _():
        sent(cs, c_s)

    @pl.when(own_context)
    def _():
        sent(cs.at[0:15], c_s)

    @pl.when(encoding)
    def _():
        a_dec.wait_send()
        sent(relay, fl_s)
        sent(xf.at[0], fw_s)
        for c in range(2):
            b_mem(c).wait_send()
        sent(kvs.at[0:62], kv_s)

    @pl.when(decoding)
    def _():
        sent(relay, fw_s)
        sent(xf.at[0, :, 0:160, :], fl_s)
        b_dec.wait_send()
        c_dec.wait_send()
        residual_out.wait_send()
        x_out(core).wait_send()
        sent(wo.at[core], wx_s)

        @pl.when(odd == 1)
        def _():
            sent(qs, q_s)

        @pl.when(odd == 0)
        def _():
            sent(acc.at[0:496], q_s)

        sent(rs.at[0:3], rs_s)


def on_device(memory, decoder_rows, gains, weights, lengths):
    bf16, f32 = jnp.bfloat16, jnp.float32
    anywhere = pl.BlockSpec(memory_space=pl.ANY)
    vmem = pl.BlockSpec(memory_space=pltpu.VMEM)
    dma = pltpu.SemaphoreType.DMA
    return pl.pallas_call(
        body,
        name="cross_attention",
        out_shape=jax.ShapeDtypeStruct((2, 64, 512), bf16),
        in_specs=[anywhere, anywhere, vmem, anywhere, pl.BlockSpec(memory_space=pltpu.SMEM)],
        out_specs=vmem,
        scratch_shapes=[
            pltpu.VMEM((4, 4096, 512), bf16),
            pltpu.VMEM((2, 4, 512, 1024), bf16),
            pltpu.VMEM((4, 2, 256, 1024), bf16),
            pltpu.VMEM((4, 2, 64, 1024), bf16),
            pltpu.VMEM((6, 2, PIECE, 1024), bf16),
            pltpu.VMEM((2, 256, 4096), bf16),
            pltpu.VMEM((64, 128, 128), bf16),
            pltpu.VMEM((2, 16, 128, 128), bf16),
            pltpu.VMEM((16, 2, 32, 128), bf16),
            pltpu.VMEM((16, 32, 128), bf16),
            pltpu.VMEM((1024, 128), bf16),
            pltpu.VMEM((1024, 128), f32),
            pltpu.VMEM((1024, 128), f32),
            pltpu.VMEM((16, 32, 128), bf16),
            pltpu.VMEM((2, 16, 32, 128), bf16),
            pltpu.VMEM((2, 128, 1024), bf16),
            pltpu.VMEM((4, 2, 64, 512), bf16),
            pltpu.VMEM((2, 2, 64, 512), bf16),
            pltpu.VMEM((2, 64, 512), bf16),
            dma,
            dma,
            dma,
            dma,
            dma,
            dma((16,)),
            dma((16,)),
            dma,
            dma,
            dma((2,)),
            dma((2,)),
            dma((2,)),
            dma((3,)),
            dma,
            dma((2,)),
            dma,
            dma,
            dma,
            dma,
            dma,
            dma,
            dma,
            dma,
            dma,
            dma,
        ],
        compiler_params=pltpu.CompilerParams(
            collective_id=0, has_side_effects=True, vmem_limit_bytes=60 << 20
        ),
    )(memory, decoder_rows, gains, weights, lengths)


def solution(mesh):
    in_specs = (
        P(None, "seq", "mp"),
        P(None, "seq", "mp"),
        P("segment", None),
        P("segment", None, None, "mp"),
        P(),
    )
    out_specs = P(None, "seq", ("segment", "mp"))
    return jax.shard_map(
        on_device, mesh=mesh, in_specs=in_specs, out_specs=out_specs, check_vma=False
    )
```

time: 472 us -> 64.9 us (0.14)
  the two profiles are of different devices: /device:TPU:7 before, /device:TPU:1 now
where the time goes in v2:
time: 64.9 us; the launch traced here: 64.7 us
  Pallas kernels  63.1 us (97%)
  local copies, waits for them, and re-layouts  1.57 us (2%)
    pallas_call x1, Pallas kernels, on_device(): pl.pallas_call(body, name='cross_attention', out_shape=jax.ShapeDtypeStru...  63.1 us
    unnamed x1, local copies, waits for them, and re-layouts  1.57 us

profile of v2, /device:TPU:1, one launch (start us, length us, event | category | flops | bytes accessed | tf_op | source)
XLA Modules:
  0.0 64.7 jit_solution(4621447183785249798)
XLA Ops:
  0.0 63.1 %cross_attention.1 = bf16[2,64,512]{2,1,0:T(8,128)(2,1)} custom-call(bf16[2,256,1024]{2,1,0:T(8,128)(2,1)} %mem.1, bf16[2,64,1024]{2,1,0:T(8,128)(2,1)} %dec.1, bf16[1,4096]{1,0:T(2,128)(2,1)} %gain.1, bf16[1,2,4096,1024]{3,2,1,0:T(8,128)(2,1)} %w.1, s32[2]{0:T(128)} %lens.1), custom_call_target="tpu_custom_call" | custom-call | tf_op jit(solution)/shard_map/cross_attention/pallas_call | solution.py:495
  63.1 1.6 %copy.7 = bf16[2,64,512]{2,1,0:T(8,128)(2,1)} copy(bf16[2,64,512]{2,1,0:T(8,128)(2,1)} %cross_attention.1) | data formatting | bytes 262144

commit v3 on v2

--- a/solution.py
+++ b/solution.py
@@ -12,9 +12,9 @@
 ROWS = 256
 SPAN = 2048
 PIECE = 16
-DIRECT = ((0, 1, 2, 3, 4), (8, 9, 10, 11, 12))
-RELAYED = (5, 6, 7, 13, 14, 15)
-ARRIVAL = ((0, 1, 2, 5, 3, 6, 4, 7), (8, 9, 10, 13, 11, 14, 12, 15))
+DIRECT = ((0, 1, 2, 3, 4), (8, 9, 10, 12, 13))
+RELAYED = (5, 6, 7, 11, 14, 15)
+ARRIVAL = ((0, 1), (2, 5), (3, 6), (4, 7)), ((8,), (9,), (10, 11), (12,)), ((13,), (14,), (15,), ())
 
 
 def seq_of(n):
@@ -23,15 +23,16 @@
 
 def body(
     mem, dec, gain, w, lens, out,
-    wbuf, wo, xf, xd, relay, xn, kvs, kvr, qs, qr, q2, acc, mx, cs, cr, cx, rs, rr, res,
-    w_sem, wo_sem, wx_s, wx_r, own_sem, gp_r, gf_r, fl_s, fw_s, gb_s, gb_r, d_s, d_r,
-    kv_s, kv_r, q_s, q_r, c_s, c_r, x_s, x_r, rs_s, rs_r, res_s, res_r,
+    wbuf, wo, xf, xd, relay, sq, st, inv, xn, pf, po, kvs, kvr, qs, qr, q2, acc, mx, cs, cr, cx, rs, rr, res,
+    w_sem, wo_sem, wx_s, wx_r, own_sem, gp_r, gf_r, fl_s, fw_s, gb_s, gb_r, st_s, st_r, d_s, d_r,
+    kv_s, kv_r, q_s, q_r, c_s, c_r, x_s, x_r, rs_s, rs_r, res_s, res_r, ring_y, ring_z,
 ):
     s = lax.axis_index("segment")
     q = lax.axis_index("seq")
     m = lax.axis_index("mp")
     across = jnp.bitwise_xor(m, 2)
     beside = jnp.bitwise_xor(m, 1)
+    corner = jnp.bitwise_xor(m, 3)
     half, core = m // 2, m % 2
     z, y = q // 4, q % 4
     slot = 4 * lax.rem(y - z + 4, 4) + z
@@ -64,11 +65,25 @@
     def o_weight_out(k):
         return remote(out_rows(k, 1 - core), wo.at[core, k], wx_s, wx_r, (1, q, beside))
 
+    bar = pltpu.get_barrier_semaphore()
+
+    def hello(*device):
+        pl.semaphore_signal(bar, inc=1, device_id=device, device_id_type=MESH)
+
+    for peer in (beside, across, corner):
+        hello(s, q, peer)
+    hello(1 - s, q, m)
+    hello(1 - s, q, across)
+    ys = [4 * z + lax.rem(y + k, 4) for k in (1, 2, 3)]
+    zs = [4 * lax.rem(z + k, 4) + y for k in (1, 2, 3)]
+    for k in ys + zs:
+        hello(s, k, m)
+
+    own_mem = pltpu.make_async_copy(mem, xf.at[m], own_sem)
+
     @pl.when(encoding)
     def _():
-        for jj in range(4):
-            for t in range(2):
-                kv_weight(jj, t).start()
+        own_mem.start()
 
     @pl.when(decoding)
     def _():
@@ -77,37 +92,36 @@
         for k in range(4):
             o_weight(k).start()
 
-    bar = pltpu.get_barrier_semaphore()
-
-    def hello(*device):
-        pl.semaphore_signal(bar, inc=1, device_id=device, device_id_type=MESH)
-
-    def greet(k, _):
-        k_odd = (k // 4) % 2 == 1
-        hello(0, k, m)
-
-        @pl.when(jnp.logical_or(encoding, jnp.logical_not(jnp.logical_and(k_odd, odd == 1))))
-        def _():
-            hello(1, k, m)
-
-        @pl.when(jnp.logical_or(k_odd, jnp.logical_and(decoding, jnp.logical_or(odd == 1, k == q))))
-        def _():
-            hello(1, k, across)
-
-        @pl.when(jnp.logical_and(decoding, jnp.logical_or(odd == 1, k == q)))
-        def _():
-            hello(0, k, across)
-
-        @pl.when(jnp.logical_and(encoding, jnp.logical_and(odd == 0, k == q)))
-        def _():
-            hello(1, k, across)
-
-        return 0
-
-    hello(s, q, beside)
-    lax.fori_loop(0, SEQ, greet, 0)
-    peers = jnp.where(encoding, jnp.where(odd == 1, 41, 42), jnp.where(odd == 1, 57, 43))
-    pl.semaphore_wait(bar, peers)
+    @pl.when(encoding)
+    def _():
+        own_mem.wait()
+        for jj in range(4):
+            for t in range(2):
+                kv_weight(lax.rem(jj + y, 4), t).start()
+        for d in range(2):
+
+            def squares(r, _, d=d):
+                rows = pl.ds(pl.multiple_of(r * 32, 32), 32)
+                part = xf[m, d, rows, :].astype(jnp.float32)
+                part = part * part
+                total = part[:, :128]
+                for k in range(1, 8):
+                    total = total + part[:, k * 128 : (k + 1) * 128]
+                sq[rows, :] = total
+                return 0
+
+            lax.fori_loop(0, 8, squares, 0)
+            st[m, d] = jnp.broadcast_to(jnp.sum(sq[...].T, axis=0, keepdims=True), (8, 256))
+
+    pl.semaphore_wait(bar, 11)
+    for k in ys:
+        pl.semaphore_signal(ring_y, inc=1, device_id=(s, k, m), device_id_type=MESH)
+
+    def tell_z():
+        pl.semaphore_wait(ring_y, 3)
+        for k in zs:
+            pl.semaphore_signal(ring_z, inc=1, device_id=(s, k, m), device_id_type=MESH)
+
 
     def piece(ref, p):
         return ref.at[:, pl.ds(p * PIECE, PIECE), :]
@@ -135,114 +149,133 @@
         there = jnp.bitwise_xor(beside, 2)
         return remote(piece(mem, p), piece(xf.at[there], p), fw_s, gf_r.at[p], (0, q, beside))
 
-    def mem_half(c):
-        return mem.at[:, pl.ds(c * 128, 128), :]
-
-    own_mem = pltpu.make_async_copy(mem, xf.at[m], own_sem)
-
-    def b_mem(c):
-        return remote(
-            mem_half(c), xf.at[m, :, pl.ds(c * 128, 128), :], gb_s.at[c], gb_r.at[c], (0, q, beside)
-        )
+    b_mem = remote(mem, xf.at[m], gb_s, gb_r, (0, q, beside))
+
+    def stats(to):
+        return remote(st.at[m], st.at[m], st_s, st_r, (0, q, to))
 
     own_dec = pltpu.make_async_copy(dec, xd.at[m], own_sem)
     a_dec = remote(dec, xd.at[m], d_s.at[0], d_r.at[0], (1, q, across))
     b_dec = remote(dec, xd.at[m], d_s.at[0], d_r.at[1], (1, q, beside))
     c_dec = remote(xd.at[across], xd.at[across], d_s.at[1], d_r.at[2], (1, q, beside))
 
-    def normalise(source, start, put):
-        total = jnp.zeros((2, PIECE, 1), jnp.float32)
-        for k in range(4):
-            part = source[k, :, pl.ds(start, PIECE), :].astype(jnp.float32)
-            total = total + jnp.sum(part * part, axis=2, keepdims=True)
-        inverse = lax.rsqrt(total * (1.0 / 4096) + EPS)
-        for k in range(4):
-            part = source[k, :, pl.ds(start, PIECE), :].astype(jnp.float32)
-            wide = part * inverse * gain[:, k * 1024 : (k + 1) * 1024].astype(jnp.float32)
-            put(slice(k * 1024, (k + 1) * 1024), wide.astype(jnp.bfloat16))
-
     low = lax.broadcasted_iota(jnp.int32, (1, 128), 1) < 64
 
     def tile_of(c, i, doc):
         return (c * SEQ + i) * 2 + doc
 
-    def kv_out(c, i, doc, device):
-        return remote(kvs.at[tile_of(c, i, doc)], kvr.at[c, q], kv_s, kv_r.at[c], device)
+    def kv_out(at, i, doc):
+        c, start, rows = at
+        tile = kvs.at[tile_of(c, i, doc), pl.ds(start, rows)]
+        return tile, kvr.at[c, q, pl.ds(start, rows)], kv_r.at[c]
 
     def unit_of(doc, i, e):
         return (0, seq_of(i), m) if doc == 0 else (1, seq_of(i), m if e % 2 == 0 else across)
 
-    def normalise_mem(p):
-        c, at = p // 8, (p % 8) * PIECE
-
-        def put(columns, value):
-            xn[c, at : at + PIECE, columns] = value[0]
-            xn[c, 128 + at : 128 + at + PIECE, columns] = value[1]
-
-        normalise(xf, p * PIECE, put)
+    def normalise_mem(p, h):
+        if p < 8:
+            at, apart = p * PIECE, 128
+        else:
+            at, apart = 256 + (p - 8) // 4 * 128 + p % 4 * PIECE, 64
+        for k in range(2):
+            columns = pl.ds(pl.multiple_of((2 * h + k) * 1024, 1024), 1024)
+            weight = gain[:, columns].astype(jnp.float32)
+            for d in range(2):
+                rows = slice(p * PIECE, (p + 1) * PIECE)
+                part = xf[2 * h + k, d, rows, :].astype(jnp.float32)
+                inverse = jnp.concatenate([inv[d, rows, :]] * 8, axis=1)
+                xn[h, at + d * apart : at + d * apart + PIECE, k * 1024 : (k + 1) * 1024] = (
+                    part * inverse * weight
+                ).astype(jnp.bfloat16)
 
     @pl.when(encoding)
     def _():
+        for to in (across, corner, beside):
+            stats(to).start()
         hop(0).start()
-        b_mem(0).start()
-        for n in range(1, 6):
+        b_mem.start()
+        hop(1).start()
+        hop(2).start()
+        a_dec.start()
+        for n in range(3, 6):
             hop(n).start()
-        a_dec.start()
-        own_mem.start()
+        pltpu.make_async_copy(st.at[0:3], st.at[0:3], st_r).wait()
+        for d in range(2):
+            total = (st[0, d] + st[1, d]) + (st[2, d] + st[3, d])
+            inverse = lax.rsqrt(total * (1.0 / 4096) + EPS)
+            inv[d] = jnp.broadcast_to(inverse[0:1, :], (128, 256)).T
+        tell_z()
+        b_mem.wait_recv()
+        for p in range(16):
+            normalise_mem(p, half)
 
         def ready(p):
             forward_in(p).wait_recv()
-            normalise_mem(p)
-
-        own_mem.wait()
-        b_mem(0).wait_recv()
-        for n, p in enumerate(ARRIVAL[0]):
+            normalise_mem(p, 1 - half)
+
+        def pass_beside(p):
             piece_in(p).wait_recv()
             forward(p).start()
-            if n >= 2:
-                ready(ARRIVAL[0][n - 2])
-        b_mem(1).start()
-        ready(ARRIVAL[0][6])
-        ready(ARRIVAL[0][7])
+
+        def rows_of(h):
+            return pl.ds(pl.multiple_of(h * 2048, 2048), 2048)
+
         pltpu.make_async_copy(wbuf, wbuf, w_sem).wait()
 
-        def project(c, jj):
+        for jj in range(4):
             j = lax.rem(jj + y, 4)
-            both = jnp.dot(xn[c], wbuf[j], preferred_element_type=jnp.float32)
+            pf[jj] = jnp.dot(xn[half], wbuf[j, rows_of(half), :], preferred_element_type=jnp.float32)
+            for p in ARRIVAL[0][jj]:
+                pass_beside(p)
+        for p in sum(ARRIVAL[0], ()):
+            ready(p)
+        pl.semaphore_wait(ring_z, 3)
+
+        def project(at, first, jj):
+            c, start, rows = at
+            j = lax.rem(jj + y, 4)
+            both = pf[jj, first : first + 2 * rows, :] + jnp.dot(
+                xn[1 - half, first : first + 2 * rows, :],
+                wbuf[j, rows_of(1 - half), :],
+                preferred_element_type=jnp.float32,
+            )
             for u in range(2):
                 key = pltpu.roll(both[:, u * 128 : (u + 1) * 128], 64, 1)
                 value = both[:, 256 + u * 128 : 256 + (u + 1) * 128]
                 for e in range(2):
                     i = 4 * j + 2 * u + e
                     tile = jnp.where(low, value, key) if e == 0 else jnp.where(low, key, value)
-                    kvs[pl.ds(tile_of(c, i, 0), 2)] = tile.astype(jnp.bfloat16).reshape(2, 128, 128)
+                    kvs[pl.ds(tile_of(c, i, 0), 2), start : start + rows] = tile.astype(
+                        jnp.bfloat16
+                    ).reshape(2, rows, 128)
             for e in range(4):
                 i = 4 * j + e
-                kv_out(c, i, 1, unit_of(1, i, e)).start()
+                tile, there, sem = kv_out(at, i, 1)
+                remote(tile, there, kv_s, sem, unit_of(1, i, e)).start()
+                tile, there, sem = kv_out(at, i, 0)
 
                 @pl.when(i != slot)
-                def _(i=i, e=e):
-                    kv_out(c, i, 0, unit_of(0, i, e)).start()
+                def _(tile=tile, there=there, sem=sem, i=i, e=e):
+                    remote(tile, there, kv_s, sem, unit_of(0, i, e)).start()
 
                 @pl.when(i == slot)
-                def _(i=i):
-                    pltpu.make_async_copy(kvs.at[tile_of(c, i, 0)], kvr.at[c, q], kv_r.at[c]).start()
-
-        waiting = []
+                def _(tile=tile, there=there, sem=sem):
+                    pltpu.make_async_copy(tile, there, sem).start()
+
         for jj in range(4):
-            project(0, jj)
-            for p in waiting:
-                ready(p)
-            waiting = ARRIVAL[1][2 * jj : 2 * jj + 2]
-            if jj == 0:
-                b_mem(1).wait_recv()
-            for p in waiting:
-                piece_in(p).wait_recv()
-                forward(p).start()
-        for p in waiting:
+            project((0, 0, 128), 0, jj)
+            for p in ARRIVAL[1][jj]:
+                pass_beside(p)
+        for p in range(8, 12):
             ready(p)
         for jj in range(4):
-            project(1, jj)
+            project((1, 0, 64), 256, jj)
+            for p in ARRIVAL[2][jj]:
+                pass_beside(p)
+        for p in range(12, 16):
+            ready(p)
+        for jj in range(4):
+            project((1, 64, 64), 384, jj)
 
     def q_out(i, doc, device):
         return remote(qs.at[i, doc], qr.at[slot], q_s, q_r, device)
@@ -263,27 +296,39 @@
             remote(piece(mem, p), relay.at[n], fl_s, gp_r.at[p], (1, q, across)).wait_recv()
             relayed(n).start()
 
-        for n in range(3):
-            pass_on(n)
+        pass_on(0)
+        tell_z()
+        pass_on(1)
+        pass_on(2)
         for p in DIRECT[1]:
             direct(p).start()
-        for n in range(3, 6):
-            pass_on(n)
         remote(dec, xd.at[across], d_s.at[0], d_r.at[0], (1, q, across)).wait_recv()
         c_dec.start()
+        pass_on(3)
+        pass_on(4)
         own_dec.wait()
         b_dec.wait_recv()
         c_dec.wait_recv()
         for p in range(4):
-
-            def put(columns, value, p=p):
-                xn[0, p * PIECE : (p + 1) * PIECE, columns] = value[0]
-                xn[0, 64 + p * PIECE : 64 + (p + 1) * PIECE, columns] = value[1]
-
-            normalise(xd, p * PIECE, put)
+            rows = slice(p * PIECE, (p + 1) * PIECE)
+            total = jnp.zeros((2, PIECE, 1), jnp.float32)
+            for k in range(4):
+                part = xd[k, :, rows, :].astype(jnp.float32)
+                total = total + jnp.sum(part * part, axis=2, keepdims=True)
+            inverse = lax.rsqrt(total * (1.0 / 4096) + EPS)
+            for k in range(4):
+                part = xd[k, :, rows, :].astype(jnp.float32)
+                wide = part * inverse * gain[:, k * 1024 : (k + 1) * 1024].astype(jnp.float32)
+                wide = wide.astype(jnp.bfloat16)
+                columns = slice((k % 2) * 1024, (k % 2 + 1) * 1024)
+                xn[k // 2, p * PIECE : (p + 1) * PIECE, columns] = wide[0]
+                xn[k // 2, 64 + p * PIECE : 64 + (p + 1) * PIECE, columns] = wide[1]
+        pass_on(5)
+        pl.semaphore_wait(ring_z, 3)
         pltpu.make_async_copy(wbuf.at[0:2], wbuf.at[0:2], w_sem).wait()
         for b in range(2):
-            made = jnp.dot(xn[0, :128, :], wbuf[b], preferred_element_type=jnp.float32)
+            made = jnp.dot(xn[0, :128, :], wbuf[b, :2048, :], preferred_element_type=jnp.float32)
+            made = made + jnp.dot(xn[1, :128, :], wbuf[b, 2048:, :], preferred_element_type=jnp.float32)
             for u in range(4):
                 pair = made[:, u * 128 : (u + 1) * 128]
                 turned = pltpu.roll(pair, 64, 1)
@@ -418,16 +463,14 @@
             )
 
         far, own = 3 - half, 2 + half
-        part = partial(core, far)
+        for k in (far, 0, 1, own):
+            po[k] = partial(core, k)
         x_out(1 - core).wait_recv()
-        part = part + partial(1 - core, far)
-        rs[far] = part.astype(jnp.bfloat16).reshape(2, 64, 512)
-        rs_out(far).start()
-        for k in range(2):
-            part = partial(0, k) + partial(1, k)
+        for k in (far, 0, 1):
+            part = po[k] + partial(1 - core, k)
             rs[k] = part.astype(jnp.bfloat16).reshape(2, 64, 512)
             rs_out(k).start()
-        part = partial(0, own) + partial(1, own)
+        part = po[own] + partial(1 - core, own)
         rr[half] = part.astype(jnp.bfloat16).reshape(2, 64, 512)
         res[...] = xd[2 + half, :, :, pl.ds(pl.multiple_of(core * 512, 512), 512)]
 
@@ -462,8 +505,8 @@
         a_dec.wait_send()
         sent(relay, fl_s)
         sent(xf.at[0], fw_s)
-        for c in range(2):
-            b_mem(c).wait_send()
+        b_mem.wait_send()
+        sent(st.at[0:3], st_s)
         sent(kvs.at[0:62], kv_s)
 
     @pl.when(decoding)
@@ -504,7 +547,12 @@
             pltpu.VMEM((4, 2, 256, 1024), bf16),
             pltpu.VMEM((4, 2, 64, 1024), bf16),
             pltpu.VMEM((6, 2, PIECE, 1024), bf16),
-            pltpu.VMEM((2, 256, 4096), bf16),
+            pltpu.VMEM((256, 128), f32),
+            pltpu.VMEM((4, 2, 8, 256), f32),
+            pltpu.VMEM((2, 256, 128), f32),
+            pltpu.VMEM((2, 512, 2048), bf16),
+            pltpu.VMEM((4, 512, 512), f32),
+            pltpu.VMEM((4, 128, 512), f32),
             pltpu.VMEM((64, 128, 128), bf16),
             pltpu.VMEM((2, 16, 128, 128), bf16),
             pltpu.VMEM((16, 2, 32, 128), bf16),
@@ -527,8 +575,10 @@
             dma((16,)),
             dma,
             dma,
-            dma((2,)),
-            dma((2,)),
+            dma,
+            dma,
+            dma,
+            dma,
             dma((2,)),
             dma((3,)),
             dma,
@@ -543,6 +593,8 @@
             dma,
             dma,
             dma,
+            pltpu.SemaphoreType.REGULAR,
+            pltpu.SemaphoreType.REGULAR,
         ],
         compiler_params=pltpu.CompilerParams(
             collective_id=0, has_side_effects=True, vmem_limit_bytes=60 << 20

time: 64.9 us -> 61.6 us (0.949)
  Pallas kernels: 63.1 us -> 59.8 us
    pallas_call x1, Pallas kernels: 63.1 us -> 59.8 us  [on_device(): pl.pallas_call(body, name='cross_attention', out_shape=jax.ShapeDtypeStru...]
where the time goes in v3:
time: 61.6 us; the launch traced here: 61.4 us
  Pallas kernels  59.8 us (97%)
  local copies, waits for them, and re-layouts  1.57 us (3%)
    pallas_call x1, Pallas kernels, on_device(): pl.pallas_call(body, name='cross_attention', out_shape=jax.ShapeDtypeStru...  59.8 us
    unnamed x1, local copies, waits for them, and re-layouts  1.57 us

profile of v3, /device:TPU:1, one launch (start us, length us, event | category | flops | bytes accessed | tf_op | source)
XLA Modules:
  0.0 61.4 jit_solution(6341831770406562481)
XLA Ops:
  0.0 59.8 %cross_attention.1 = bf16[2,64,512]{2,1,0:T(8,128)(2,1)} custom-call(bf16[2,256,1024]{2,1,0:T(8,128)(2,1)} %mem.1, bf16[2,64,1024]{2,1,0:T(8,128)(2,1)} %dec.1, bf16[1,4096]{1,0:T(2,128)(2,1)} %gain.1, bf16[1,2,4096,1024]{3,2,1,0:T(8,128)(2,1)} %w.1, s32[2]{0:T(128)} %lens.1), custom_call_target="tpu_custom_call" | custom-call | tf_op jit(solution)/shard_map/cross_attention/pallas_call | solution.py:538
  59.8 1.6 %copy.7 = bf16[2,64,512]{2,1,0:T(8,128)(2,1)} copy(bf16[2,64,512]{2,1,0:T(8,128)(2,1)} %cross_attention.1) | data formatting | bytes 262144

commit v4 on v3

--- a/solution.py
+++ b/solution.py
@@ -10,11 +10,10 @@
 MASKED = -1e30
 SEQ = 16
 ROWS = 256
-SPAN = 2048
 PIECE = 16
-DIRECT = ((0, 1, 2, 3, 4), (8, 9, 10, 12, 13))
-RELAYED = (5, 6, 7, 11, 14, 15)
-ARRIVAL = ((0, 1), (2, 5), (3, 6), (4, 7)), ((8,), (9,), (10, 11), (12,)), ((13,), (14,), (15,), ())
+DIRECT = (tuple(range(8)), (12, 13, 14, 15))
+RELAYED = (8, 9, 10, 11)
+ARRIVAL = ((0, 1), (2,), (3,), (4,)), ((), (5,), (), (6,)), ((), (8,), (9,), (10, 11)), ((12,), (13,), (14,), (15,))
 
 
 def seq_of(n):
@@ -70,10 +69,10 @@
     def hello(*device):
         pl.semaphore_signal(bar, inc=1, device_id=device, device_id_type=MESH)
 
-    for peer in (beside, across, corner):
+    for peer in (beside, across):
         hello(s, q, peer)
-    hello(1 - s, q, m)
-    hello(1 - s, q, across)
+    for peer in (m, across, corner):
+        hello(1 - s, q, peer)
     ys = [4 * z + lax.rem(y + k, 4) for k in (1, 2, 3)]
     zs = [4 * lax.rem(z + k, 4) + y for k in (1, 2, 3)]
     for k in ys + zs:
@@ -81,9 +80,14 @@
 
     own_mem = pltpu.make_async_copy(mem, xf.at[m], own_sem)
 
+    own_mem.start()
+    own_mem.wait()
+
     @pl.when(encoding)
     def _():
-        own_mem.start()
+        for jj in range(4):
+            for t in range(2):
+                kv_weight(lax.rem(slot // 4 + jj, 4), t).start()
 
     @pl.when(decoding)
     def _():
@@ -92,26 +96,20 @@
         for k in range(4):
             o_weight(k).start()
 
-    @pl.when(encoding)
-    def _():
-        own_mem.wait()
-        for jj in range(4):
-            for t in range(2):
-                kv_weight(lax.rem(jj + y, 4), t).start()
-        for d in range(2):
-
-            def squares(r, _, d=d):
-                rows = pl.ds(pl.multiple_of(r * 32, 32), 32)
-                part = xf[m, d, rows, :].astype(jnp.float32)
-                part = part * part
-                total = part[:, :128]
-                for k in range(1, 8):
-                    total = total + part[:, k * 128 : (k + 1) * 128]
-                sq[rows, :] = total
-                return 0
-
-            lax.fori_loop(0, 8, squares, 0)
-            st[m, d] = jnp.broadcast_to(jnp.sum(sq[...].T, axis=0, keepdims=True), (8, 256))
+    for d in range(2):
+
+        def squares(r, _, d=d):
+            rows = pl.ds(pl.multiple_of(r * 32, 32), 32)
+            part = xf[m, d, rows, :].astype(jnp.float32)
+            part = part * part
+            total = part[:, :128]
+            for k in range(1, 8):
+                total = total + part[:, k * 128 : (k + 1) * 128]
+            sq[rows, :] = total
+            return 0
+
+        lax.fori_loop(0, 8, squares, 0)
+        st[m, d] = jnp.broadcast_to(jnp.sum(sq[...].T, axis=0, keepdims=True), (8, 256))
 
     pl.semaphore_wait(bar, 11)
     for k in ys:
@@ -167,16 +165,13 @@
     def kv_out(at, i, doc):
         c, start, rows = at
         tile = kvs.at[tile_of(c, i, doc), pl.ds(start, rows)]
-        return tile, kvr.at[c, q, pl.ds(start, rows)], kv_r.at[c]
+        return tile, kvr.at[c, q, pl.ds(start, rows)], kv_r.at[c * (1 + start // 64)]
 
     def unit_of(doc, i, e):
-        return (0, seq_of(i), m) if doc == 0 else (1, seq_of(i), m if e % 2 == 0 else across)
+        return (0, seq_of(i), m) if doc == 0 else (1, seq_of(i), jnp.where(e % 2 == 0, m, across))
 
     def normalise_mem(p, h):
-        if p < 8:
-            at, apart = p * PIECE, 128
-        else:
-            at, apart = 256 + (p - 8) // 4 * 128 + p % 4 * PIECE, 64
+        at = p // 4 * 128 + p % 4 * PIECE
         for k in range(2):
             columns = pl.ds(pl.multiple_of((2 * h + k) * 1024, 1024), 1024)
             weight = gain[:, columns].astype(jnp.float32)
@@ -184,21 +179,15 @@
                 rows = slice(p * PIECE, (p + 1) * PIECE)
                 part = xf[2 * h + k, d, rows, :].astype(jnp.float32)
                 inverse = jnp.concatenate([inv[d, rows, :]] * 8, axis=1)
-                xn[h, at + d * apart : at + d * apart + PIECE, k * 1024 : (k + 1) * 1024] = (
+                xn[h, at + d * 64 : at + d * 64 + PIECE, k * 1024 : (k + 1) * 1024] = (
                     part * inverse * weight
                 ).astype(jnp.bfloat16)
 
     @pl.when(encoding)
     def _():
-        for to in (across, corner, beside):
-            stats(to).start()
-        hop(0).start()
+        stats(beside).start()
+        a_dec.start()
         b_mem.start()
-        hop(1).start()
-        hop(2).start()
-        a_dec.start()
-        for n in range(3, 6):
-            hop(n).start()
         pltpu.make_async_copy(st.at[0:3], st.at[0:3], st_r).wait()
         for d in range(2):
             total = (st[0, d] + st[1, d]) + (st[2, d] + st[3, d])
@@ -208,6 +197,8 @@
         b_mem.wait_recv()
         for p in range(16):
             normalise_mem(p, half)
+        for n in range(4):
+            hop(n).start()
 
         def ready(p):
             forward_in(p).wait_recv()
@@ -223,17 +214,17 @@
         pltpu.make_async_copy(wbuf, wbuf, w_sem).wait()
 
         for jj in range(4):
-            j = lax.rem(jj + y, 4)
+            j = lax.rem(slot // 4 + jj, 4)
             pf[jj] = jnp.dot(xn[half], wbuf[j, rows_of(half), :], preferred_element_type=jnp.float32)
             for p in ARRIVAL[0][jj]:
                 pass_beside(p)
-        for p in sum(ARRIVAL[0], ()):
+        for p in range(4):
             ready(p)
         pl.semaphore_wait(ring_z, 3)
 
         def project(at, first, jj):
             c, start, rows = at
-            j = lax.rem(jj + y, 4)
+            j = lax.rem(slot // 4 + jj, 4)
             both = pf[jj, first : first + 2 * rows, :] + jnp.dot(
                 xn[1 - half, first : first + 2 * rows, :],
                 wbuf[j, rows_of(1 - half), :],
@@ -248,34 +239,33 @@
                     kvs[pl.ds(tile_of(c, i, 0), 2), start : start + rows] = tile.astype(
                         jnp.bfloat16
                     ).reshape(2, rows, 128)
-            for e in range(4):
+
+            def send(e, doc):
                 i = 4 * j + e
-                tile, there, sem = kv_out(at, i, 1)
-                remote(tile, there, kv_s, sem, unit_of(1, i, e)).start()
-                tile, there, sem = kv_out(at, i, 0)
-
-                @pl.when(i != slot)
-                def _(tile=tile, there=there, sem=sem, i=i, e=e):
-                    remote(tile, there, kv_s, sem, unit_of(0, i, e)).start()
-
-                @pl.when(i == slot)
-                def _(tile=tile, there=there, sem=sem):
-                    pltpu.make_async_copy(tile, there, sem).start()
-
-        for jj in range(4):
-            project((0, 0, 128), 0, jj)
-            for p in ARRIVAL[1][jj]:
-                pass_beside(p)
-        for p in range(8, 12):
-            ready(p)
-        for jj in range(4):
-            project((1, 0, 64), 256, jj)
-            for p in ARRIVAL[2][jj]:
-                pass_beside(p)
-        for p in range(12, 16):
-            ready(p)
-        for jj in range(4):
-            project((1, 64, 64), 384, jj)
+                remote(*kv_out(at, i, doc)[:2], kv_s, kv_out(at, i, doc)[2], unit_of(doc, i, e)).start()
+
+            for k in range(4):
+                e = lax.rem(z + k, 4)
+                if jj + k:
+                    send(e, 0)
+                else:
+                    pltpu.make_async_copy(*kv_out(at, slot, 0)).start()
+                send(e, 1)
+
+        for quarter in range(4):
+            for jj in range(4):
+                project((quarter // 2, quarter % 2 * 64, 64), quarter * 128, jj)
+                if quarter < 3:
+                    for p in ARRIVAL[quarter + 1][jj]:
+                        pass_beside(p)
+            if quarter == 0:
+                ready(4)
+                pass_beside(7)
+                for p in range(5, 8):
+                    ready(p)
+            elif quarter < 3:
+                for p in range(4 * quarter + 4, 4 * quarter + 8):
+                    ready(p)
 
     def q_out(i, doc, device):
         return remote(qs.at[i, doc], qr.at[slot], q_s, q_r, device)
@@ -286,6 +276,8 @@
 
     @pl.when(decoding)
     def _():
+        stats(across).start()
+        stats(corner).start()
         for p in DIRECT[0]:
             direct(p).start()
         own_dec.start()
@@ -296,16 +288,9 @@
             remote(piece(mem, p), relay.at[n], fl_s, gp_r.at[p], (1, q, across)).wait_recv()
             relayed(n).start()
 
-        pass_on(0)
-        tell_z()
-        pass_on(1)
-        pass_on(2)
-        for p in DIRECT[1]:
-            direct(p).start()
         remote(dec, xd.at[across], d_s.at[0], d_r.at[0], (1, q, across)).wait_recv()
         c_dec.start()
-        pass_on(3)
-        pass_on(4)
+        tell_z()
         own_dec.wait()
         b_dec.wait_recv()
         c_dec.wait_recv()
@@ -323,8 +308,9 @@
                 columns = slice((k % 2) * 1024, (k % 2 + 1) * 1024)
                 xn[k // 2, p * PIECE : (p + 1) * PIECE, columns] = wide[0]
                 xn[k // 2, 64 + p * PIECE : 64 + (p + 1) * PIECE, columns] = wide[1]
-        pass_on(5)
         pl.semaphore_wait(ring_z, 3)
+        pass_on(0)
+        pass_on(1)
         pltpu.make_async_copy(wbuf.at[0:2], wbuf.at[0:2], w_sem).wait()
         for b in range(2):
             made = jnp.dot(xn[0, :128, :], wbuf[b, :2048, :], preferred_element_type=jnp.float32)
@@ -337,24 +323,36 @@
                     first, second = (pair, turned) if e == 0 else (turned, pair)
                     tile = jnp.where(low, first[:, 0], second[:, 1])
                     qs[2 * (4 * b + u) + e] = tile.astype(jnp.bfloat16)
-            for i in range(8 * b, 8 * b + 8):
-                q_out(i, 0, unit_of(0, i, i)).start()
-                if i % 2 == 1:
-                    q_out(i, 1, unit_of(1, i, i)).start()
+        pass_on(2)
+        pass_on(3)
+        for jj in range(4):
+            for k in range(4):
+                e = lax.rem(z + k, 4)
+                i = 4 * lax.rem(slot // 4 + jj, 4) + e
+                q_out(i, 0, unit_of(0, i, e)).start()
+                if jj + k:
+                    q_out(i, 1, unit_of(1, i, e)).start()
                 else:
 
-                    @pl.when(slot != i)
-                    def _(i=i):
-                        q_out(i, 1, unit_of(1, i, i)).start()
-
-                    @pl.when(slot == i)
-                    def _(i=i):
-                        pltpu.make_async_copy(qs.at[i, 1], qr.at[slot], q_r).start()
+                    @pl.when(odd == 1)
+                    def _(i=i, e=e):
+                        q_out(i, 1, unit_of(1, i, e)).start()
+
+                    @pl.when(odd == 0)
+                    def _():
+                        pltpu.make_async_copy(qs.at[slot, 1], qr.at[slot], q_r).start()
+
+        for p in DIRECT[1]:
+            direct(p).start()
+
+    pltpu.make_async_copy(qr, qr, q_r).wait()
+
+    @pl.when(decoding)
+    def _():
         residual_out.start()
         for k in range(4):
             o_weight_out(k).start()
 
-    pltpu.make_async_copy(qr, qr, q_r).wait()
     lane = lax.broadcasted_iota(jnp.int32, (1, 128), 1)
     key_half = jnp.where(odd == 1, 0, 1)
     key_lane = (lane // 64) == key_half
@@ -366,28 +364,33 @@
     q2[...] = jnp.where(key_lane, placed, 0.0).astype(jnp.bfloat16)
     length = lens[s]
     one = jnp.bfloat16(1)
-    column = lax.broadcasted_iota(jnp.int32, (1, SPAN), 1)
-    within = (column // 128) * 256 + column % 128
-
-    def kv_wait(c):
-        pltpu.make_async_copy(kvr.at[c], kvr.at[c], kv_r.at[c]).wait()
-
-    def score(c, rows):
+    passes = ((0, 0, 128), (1, 0, 64), (1, 64, 64))
+
+    def keys(at):
+        c, start, rows = at
+        return kvr[c, :, start : start + rows, :].reshape(SEQ * rows, 128)
+
+    def kv_wait(n):
+        c, start, rows = passes[n]
+        part = kvr.at[c, :, pl.ds(start, rows), :]
+        pltpu.make_async_copy(part, part, kv_r.at[n]).wait()
+
+    def score(at, rows):
         return lax.dot_general(
-            q2[rows, :],
-            kvr[c].reshape(SPAN, 128),
-            (((1,), (1,)), ((), ())),
-            preferred_element_type=jnp.float32,
+            q2[rows, :], keys(at), (((1,), (1,)), ((), ())), preferred_element_type=jnp.float32
         )
 
-    def weigh(c, scores, before):
-        scores = jnp.where(within + c * 128 < length, scores, MASKED)
+    def weigh(at, scores, before):
+        c, start, rows = at
+        column = lax.broadcasted_iota(jnp.int32, (1, SEQ * rows), 1)
+        position = column // rows * 256 + c * 128 + start + column % rows
+        scores = jnp.where(position < length, scores, MASKED)
         top = jnp.max(scores, axis=1, keepdims=True)
         top = jnp.broadcast_to(top, (ROWS, 128)) if before is None else jnp.maximum(before, top)
-        probs = jnp.exp(scores - jnp.concatenate([top] * (SPAN // 128), axis=1)).astype(jnp.bfloat16)
+        probs = jnp.exp(scores - jnp.concatenate([top] * (SEQ * rows // 128), axis=1))
         mixed = jnp.dot(
-            probs,
-            jnp.where(key_lane, one, kvr[c].reshape(SPAN, 128)),
+            probs.astype(jnp.bfloat16),
+            jnp.where(key_lane, one, keys(at)),
             preferred_element_type=jnp.float32,
         )
         return top, mixed
@@ -396,42 +399,48 @@
         return pl.ds(pl.multiple_of(r * ROWS, ROWS), ROWS)
 
     blocks = 1024 // ROWS
-    kv_wait(0)
-    scores = score(0, block(0))
-    for r in range(blocks):
-        following = score(0, block(r + 1)) if r + 1 < blocks else None
-        top, mixed = weigh(0, scores, None)
-        mx[block(r), :] = top
-        acc[block(r), :] = mixed
-        scores = following
+    for n in range(2):
+        kv_wait(n)
+        scores = score(passes[n], block(0))
+        for r in range(blocks):
+            following = score(passes[n], block(r + 1)) if r + 1 < blocks else None
+            before = mx[block(r), :] if n else None
+            top, mixed = weigh(passes[n], scores, before)
+            if n:
+                mixed = acc[block(r), :] * jnp.exp(before - top) + mixed
+            mx[block(r), :] = top
+            acc[block(r), :] = mixed
+            scores = following
 
     def c_out(k):
         return remote(cs.at[k], cr.at[s, slot], c_s, c_r, (1, seq_of(k), group))
 
     own_context = jnp.logical_and(decoding, odd == 0)
 
-    kv_wait(1)
-    order = [lax.rem(r + y, blocks) for r in range(blocks)]
-    scores = score(1, block(order[0]))
+    kv_wait(2)
+    order = [lax.rem(slot // 4 + r, blocks) for r in range(blocks)]
+    scores = score(passes[2], block(order[0]))
     for n, r in enumerate(order):
-        following = score(1, block(order[n + 1])) if n + 1 < blocks else None
+        following = score(passes[2], block(order[n + 1])) if n + 1 < blocks else None
         before = mx[block(r), :]
-        top, mixed = weigh(1, scores, before)
+        top, mixed = weigh(passes[2], scores, before)
         mixed = acc[block(r), :] * jnp.exp(before - top) + mixed
         context = mixed / pltpu.roll(mixed, 64, 1)
         context = jnp.where(key_lane, pltpu.roll(context, 64, 1), context).reshape(4, 2, 32, 128)
         cs[pl.ds(r * 4, 4)] = jnp.where(low, context[:, 0], context[:, 1]).astype(jnp.bfloat16)
         for k in range(4):
-            to = r * 4 + k
-            mine = jnp.logical_and(own_context, slot == to)
-
-            @pl.when(mine)
-            def _():
-                pltpu.make_async_copy(cs.at[slot], cr.at[1, slot], c_r).start()
-
-            @pl.when(jnp.logical_not(mine))
-            def _(to=to):
+            to = 4 * r + lax.rem(z + k, 4)
+            if n + k:
                 c_out(to).start()
+            else:
+
+                @pl.when(jnp.logical_not(own_context))
+                def _(to=to):
+                    c_out(to).start()
+
+                @pl.when(own_context)
+                def _():
+                    pltpu.make_async_copy(cs.at[slot], cr.at[1, slot], c_r).start()
 
         scores = following
 
@@ -463,14 +472,14 @@
             )
 
         far, own = 3 - half, 2 + half
-        for k in (far, 0, 1, own):
+        for k in (far, 0):
             po[k] = partial(core, k)
         x_out(1 - core).wait_recv()
-        for k in (far, 0, 1):
-            part = po[k] + partial(1 - core, k)
+        for n, k in enumerate((far, 0, 1)):
+            part = (po[k] if n < 2 else partial(core, k)) + partial(1 - core, k)
             rs[k] = part.astype(jnp.bfloat16).reshape(2, 64, 512)
             rs_out(k).start()
-        part = po[own] + partial(1 - core, own)
+        part = partial(core, own) + partial(1 - core, own)
         rr[half] = part.astype(jnp.bfloat16).reshape(2, 64, 512)
         res[...] = xd[2 + half, :, :, pl.ds(pl.multiple_of(core * 512, 512), 512)]
 
@@ -506,13 +515,14 @@
         sent(relay, fl_s)
         sent(xf.at[0], fw_s)
         b_mem.wait_send()
-        sent(st.at[0:3], st_s)
+        sent(st.at[0], st_s)
         sent(kvs.at[0:62], kv_s)
 
     @pl.when(decoding)
     def _():
         sent(relay, fw_s)
-        sent(xf.at[0, :, 0:160, :], fl_s)
+        sent(st.at[0:2], st_s)
+        sent(xf.at[0, :, 0:192, :], fl_s)
         b_dec.wait_send()
         c_dec.wait_send()
         residual_out.wait_send()
@@ -546,7 +556,7 @@
             pltpu.VMEM((2, 4, 512, 1024), bf16),
             pltpu.VMEM((4, 2, 256, 1024), bf16),
             pltpu.VMEM((4, 2, 64, 1024), bf16),
-            pltpu.VMEM((6, 2, PIECE, 1024), bf16),
+            pltpu.VMEM((4, 2, PIECE, 1024), bf16),
             pltpu.VMEM((256, 128), f32),
             pltpu.VMEM((4, 2, 8, 256), f32),
             pltpu.VMEM((2, 256, 128), f32),
@@ -582,7 +592,7 @@
             dma((2,)),
             dma((3,)),
             dma,
-            dma((2,)),
+            dma((3,)),
             dma,
             dma,
             dma,

time: 61.6 us -> 59.1 us (0.959)
  Pallas kernels: 59.8 us -> 57.3 us
    pallas_call x1, Pallas kernels: 59.8 us -> 57.3 us  [on_device(): pl.pallas_call(body, name='cross_attention', out_shape=jax.ShapeDtypeStru...]
where the time goes in v4:
time: 59.1 us; the launch traced here: 58.9 us
  Pallas kernels  57.3 us (97%)
  local copies, waits for them, and re-layouts  1.57 us (3%)
    pallas_call x1, Pallas kernels, on_device(): pl.pallas_call(body, name='cross_attention', out_shape=jax.ShapeDtypeStru...  57.3 us
    unnamed x1, local copies, waits for them, and re-layouts  1.57 us

profile of v4, /device:TPU:1, one launch (start us, length us, event | category | flops | bytes accessed | tf_op | source)
XLA Modules:
  0.0 58.9 jit_solution(6047465848967266237)
XLA Ops:
  0.0 57.3 %cross_attention.1 = bf16[2,64,512]{2,1,0:T(8,128)(2,1)} custom-call(bf16[2,256,1024]{2,1,0:T(8,128)(2,1)} %mem.1, bf16[2,64,1024]{2,1,0:T(8,128)(2,1)} %dec.1, bf16[1,4096]{1,0:T(2,128)(2,1)} %gain.1, bf16[1,2,4096,1024]{3,2,1,0:T(8,128)(2,1)} %w.1, s32[2]{0:T(128)} %lens.1), custom_call_target="tpu_custom_call" | custom-call | tf_op jit(solution)/shard_map/cross_attention/pallas_call | solution.py:548
  57.3 1.6 %copy.7 = bf16[2,64,512]{2,1,0:T(8,128)(2,1)} copy(bf16[2,64,512]{2,1,0:T(8,128)(2,1)} %cross_attention.1) | data formatting | bytes 262144

commit v5 on v4

--- a/solution.py
+++ b/solution.py
@@ -266,6 +266,13 @@
             elif quarter < 3:
                 for p in range(4 * quarter + 4, 4 * quarter + 8):
                     ready(p)
+
+    def turned_rows(k):
+        return pl.ds(pl.multiple_of(k * 1024, 1024), 1024)
+
+    def turn(c):
+        for k in range(4):
+            wbuf[2 + c, turned_rows(k), :] = wo[c, k].T
 
     def q_out(i, doc, device):
         return remote(qs.at[i, doc], qr.at[slot], q_s, q_r, device)
@@ -344,6 +351,8 @@
 
         for p in DIRECT[1]:
             direct(p).start()
+        pltpu.make_async_copy(wo.at[core], wo.at[core], wo_sem).wait()
+        turn(core)
 
     pltpu.make_async_copy(qr, qr, q_r).wait()
 
@@ -452,6 +461,8 @@
 
     @pl.when(decoding)
     def _():
+        remote(wo.at[core], wo.at[1 - core], wx_s, wx_r, (1, q, beside)).wait_recv()
+        turn(1 - core)
         pltpu.make_async_copy(cr, cr, c_r).wait()
         for d in range(2):
             for t in range(8):
@@ -463,23 +474,19 @@
                 cx[core, d * 64 : d * 64 + 32, at] = upper.astype(jnp.bfloat16)
                 cx[core, d * 64 + 32 : d * 64 + 64, at] = lower.astype(jnp.bfloat16)
         x_out(core).start()
-        pltpu.make_async_copy(wo.at[core], wo.at[core], wo_sem).wait()
-        remote(wo.at[core], wo.at[1 - core], wx_s, wx_r, (1, q, beside)).wait_recv()
 
         def partial(c, k):
-            return lax.dot_general(
-                cx[c], wo[c, k], (((1,), (1,)), ((), ())), preferred_element_type=jnp.float32
-            )
+            return jnp.dot(cx[c], wbuf[2 + c, turned_rows(k), :], preferred_element_type=jnp.float32)
 
         far, own = 3 - half, 2 + half
-        for k in (far, 0):
+        for k in (0, far, 1, own):
             po[k] = partial(core, k)
         x_out(1 - core).wait_recv()
-        for n, k in enumerate((far, 0, 1)):
-            part = (po[k] if n < 2 else partial(core, k)) + partial(1 - core, k)
+        for k in (0, far, 1):
+            part = po[k] + partial(1 - core, k)
             rs[k] = part.astype(jnp.bfloat16).reshape(2, 64, 512)
             rs_out(k).start()
-        part = partial(core, own) + partial(1 - core, own)
+        part = po[own] + partial(1 - core, own)
         rr[half] = part.astype(jnp.bfloat16).reshape(2, 64, 512)
         res[...] = xd[2 + half, :, :, pl.ds(pl.multiple_of(core * 512, 512), 512)]
 

time: 59.1 us -> 57.8 us (0.978)
  the two profiles are of different devices: /device:TPU:1 before, /device:TPU:7 now
where the time goes in v5:
time: 57.8 us; the launch traced here: 57.6 us
  Pallas kernels  56 us (97%)
  local copies, waits for them, and re-layouts  1.57 us (3%)
    pallas_call x1, Pallas kernels, on_device(): pl.pallas_call(body, name='cross_attention', out_shape=jax.ShapeDtypeStru...  56 us
    unnamed x1, local copies, waits for them, and re-layouts  1.57 us

profile of v5, /device:TPU:7, one launch (start us, length us, event | category | flops | bytes accessed | tf_op | source)
XLA Modules:
  0.0 57.6 jit_solution(1409476027748482813)
XLA Ops:
  0.0 56.0 %cross_attention.1 = bf16[2,64,512]{2,1,0:T(8,128)(2,1)} custom-call(bf16[2,256,1024]{2,1,0:T(8,128)(2,1)} %mem.1, bf16[2,64,1024]{2,1,0:T(8,128)(2,1)} %dec.1, bf16[1,4096]{1,0:T(2,128)(2,1)} %gain.1, bf16[1,2,4096,1024]{3,2,1,0:T(8,128)(2,1)} %w.1, s32[2]{0:T(128)} %lens.1), custom_call_target="tpu_custom_call" | custom-call | tf_op jit(solution)/shard_map/cross_attention/pallas_call | solution.py:555
  56.0 1.6 %copy.7 = bf16[2,64,512]{2,1,0:T(8,128)(2,1)} copy(bf16[2,64,512]{2,1,0:T(8,128)(2,1)} %cross_attention.1) | data formatting | bytes 262144

commit v6 on v5

--- a/solution.py
+++ b/solution.py
@@ -428,12 +428,9 @@
 
     kv_wait(2)
     order = [lax.rem(slot // 4 + r, blocks) for r in range(blocks)]
-    scores = score(passes[2], block(order[0]))
-    for n, r in enumerate(order):
-        following = score(passes[2], block(order[n + 1])) if n + 1 < blocks else None
-        before = mx[block(r), :]
-        top, mixed = weigh(passes[2], scores, before)
-        mixed = acc[block(r), :] * jnp.exp(before - top) + mixed
+
+    def finish(n, mixed):
+        r = order[n]
         context = mixed / pltpu.roll(mixed, 64, 1)
         context = jnp.where(key_lane, pltpu.roll(context, 64, 1), context).reshape(4, 2, 32, 128)
         cs[pl.ds(r * 4, 4)] = jnp.where(low, context[:, 0], context[:, 1]).astype(jnp.bfloat16)
@@ -451,7 +448,17 @@
                 def _():
                     pltpu.make_async_copy(cs.at[slot], cr.at[1, slot], c_r).start()
 
-        scores = following
+    scores = score(passes[2], block(order[0]))
+    mixed = None
+    for n, r in enumerate(order):
+        following = score(passes[2], block(order[n + 1])) if n + 1 < blocks else None
+        before = mx[block(r), :]
+        top, added = weigh(passes[2], scores, before)
+        added = acc[block(r), :] * jnp.exp(before - top) + added
+        if n:
+            finish(n - 1, mixed)
+        mixed, scores = added, following
+    finish(blocks - 1, mixed)
 
     def x_out(c):
         return remote(cx.at[c], cx.at[c], x_s, x_r, (1, q, beside))

time: 57.8 us -> 57.9 us (level)
  no operation moved by 1% of the time
where the time goes in v6:
time: 57.9 us; the launch traced here: 57.7 us
  Pallas kernels  56.1 us (97%)
  local copies, waits for them, and re-layouts  1.57 us (3%)
    pallas_call x1, Pallas kernels, on_device(): pl.pallas_call(body, name='cross_attention', out_shape=jax.ShapeDtypeStru...  56.1 us
    unnamed x1, local copies, waits for them, and re-layouts  1.57 us

profile of v6, /device:TPU:7, one launch (start us, length us, event | category | flops | bytes accessed | tf_op | source)
XLA Modules:
  0.0 57.7 jit_solution(12058976317815539678)
XLA Ops:
  0.0 56.1 %cross_attention.1 = bf16[2,64,512]{2,1,0:T(8,128)(2,1)} custom-call(bf16[2,256,1024]{2,1,0:T(8,128)(2,1)} %mem.1, bf16[2,64,1024]{2,1,0:T(8,128)(2,1)} %dec.1, bf16[1,4096]{1,0:T(2,128)(2,1)} %gain.1, bf16[1,2,4096,1024]{3,2,1,0:T(8,128)(2,1)} %w.1, s32[2]{0:T(128)} %lens.1), custom_call_target="tpu_custom_call" | custom-call | tf_op jit(solution)/shard_map/cross_attention/pallas_call | solution.py:562
  56.1 1.6 %copy.7 = bf16[2,64,512]{2,1,0:T(8,128)(2,1)} copy(bf16[2,64,512]{2,1,0:T(8,128)(2,1)} %cross_attention.1) | data formatting | bytes 262144

commit v7 on v6

--- a/solution.py
+++ b/solution.py
@@ -222,14 +222,18 @@
             ready(p)
         pl.semaphore_wait(ring_z, 3)
 
-        def project(at, first, jj):
-            c, start, rows = at
+        def multiply(at, first, jj):
+            rows = at[2]
             j = lax.rem(slot // 4 + jj, 4)
-            both = pf[jj, first : first + 2 * rows, :] + jnp.dot(
+            return pf[jj, first : first + 2 * rows, :] + jnp.dot(
                 xn[1 - half, first : first + 2 * rows, :],
                 wbuf[j, rows_of(1 - half), :],
                 preferred_element_type=jnp.float32,
             )
+
+        def deliver(at, jj, both):
+            c, start, rows = at
+            j = lax.rem(slot // 4 + jj, 4)
             for u in range(2):
                 key = pltpu.roll(both[:, u * 128 : (u + 1) * 128], 64, 1)
                 value = both[:, 256 + u * 128 : 256 + (u + 1) * 128]
@@ -253,11 +257,16 @@
                 send(e, 1)
 
         for quarter in range(4):
+            at, first = (quarter // 2, quarter % 2 * 64, 64), quarter * 128
+            both = multiply(at, first, 0)
             for jj in range(4):
-                project((quarter // 2, quarter % 2 * 64, 64), quarter * 128, jj)
+                ahead = multiply(at, first, jj + 1) if quarter == 3 and jj < 3 else None
+                deliver(at, jj, both)
                 if quarter < 3:
                     for p in ARRIVAL[quarter + 1][jj]:
                         pass_beside(p)
+                if jj < 3:
+                    both = multiply(at, first, jj + 1) if ahead is None else ahead
             if quarter == 0:
                 ready(4)
                 pass_beside(7)

time: 57.9 us -> 58.1 us (level)
  no operation moved by 1% of the time
where the time goes in v7:
time: 58.1 us; the launch traced here: 57.8 us
  Pallas kernels  56.3 us (97%)
  local copies, waits for them, and re-layouts  1.57 us (3%)
    pallas_call x1, Pallas kernels, on_device(): pl.pallas_call(body, name='cross_attention', out_shape=jax.ShapeDtypeStru...  56.3 us
    unnamed x1, local copies, waits for them, and re-layouts  1.57 us

profile of v7, /device:TPU:7, one launch (start us, length us, event | category | flops | bytes accessed | tf_op | source)
XLA Modules:
  0.0 57.8 jit_solution(9236520851347773854)
XLA Ops:
  0.0 56.3 %cross_attention.1 = bf16[2,64,512]{2,1,0:T(8,128)(2,1)} custom-call(bf16[2,256,1024]{2,1,0:T(8,128)(2,1)} %mem.1, bf16[2,64,1024]{2,1,0:T(8,128)(2,1)} %dec.1, bf16[1,4096]{1,0:T(2,128)(2,1)} %gain.1, bf16[1,2,4096,1024]{3,2,1,0:T(8,128)(2,1)} %w.1, s32[2]{0:T(128)} %lens.1), custom_call_target="tpu_custom_call" | custom-call | tf_op jit(solution)/shard_map/cross_attention/pallas_call | solution.py:571
  56.3 1.6 %copy.7 = bf16[2,64,512]{2,1,0:T(8,128)(2,1)} copy(bf16[2,64,512]{2,1,0:T(8,128)(2,1)} %cross_attention.1) | data formatting | bytes 262144
